TPU v7x, 128 devices: a whole 4x4x4 slice. The times are simulated.
128 devices in a mesh: tok: 16 (over x_lo, z, core), cell: 8 (over y, x_hi).
Axes of the slice: x: 4 (x_hi: 2, x_lo: 2; x = x_hi * 2 + x_lo), y: 4, z: 4, core: 2. Of those that a mesh axis runs over, the one named last changes fastest.
Arguments:
- activations: bfloat16 [16384, 4096], P('tok'), may hold values from -6 to 6
- out_grads: bfloat16 [16384, 1024], P('tok'), may hold values from -6 to 6
- query_ids: int32 [16384], P('tok'), may hold values from 0 to 511
- live: int32 [16], P('tok'), may hold values from 256 to 1024, as said below
- proj_in: bfloat16 [4096, 64], P(None, 'cell'), may hold values from -0.09375 to 0.09375
- proj_out: bfloat16 [1024, 32], replicated, may hold values from -0.1875 to 0.1875
- whitener: bfloat16 [2048, 2048], P('cell')
- stores: bfloat16 [196608, 2048], P(('tok', 'cell')), may hold values from -0.023925781 to 0.023925781
Outputs:
- scores: float32 [512, 196608], P(None, ('tok', 'cell'))
Inputs may be any that keep to these rules, and one draw needn't show every extreme that they name: `live`: each entry is a count of valid tokens of one block of 1024; some block is full in every draw.
All inputs are finite; a program needn't handle non-finite values.
Results may differ from a plain program's by a relative error of at most 0.005.
Values may be sent and summed in bfloat16 or wider, within the bound.
No kernel may reach another device: no remote copies, remote signals or barrier semaphores. Data moves between devices by JAX's collectives and lax.ppermute only.
A program may use at most 64 MiB of HBM per device.

v0:
```python
import jax
import jax.numpy as jnp
from jax import lax
from jax.experimental import pallas as pl
from jax.experimental.pallas import tpu as pltpu
from jax.sharding import PartitionSpec as P

Q = 512
N_X, N_Z, N_CORE, N_Y, N_XH = 2, 4, 2, 4, 2
N_TOK = N_X * N_Z * N_CORE
BLOCK = Q // N_TOK
AXES = ("tok", "cell")
NT = (((1,), (1,)), ((), ()))


PLACES = [
    (x, z, core, y, xh)
    for x in range(N_X)
    for z in range(N_Z)
    for core in range(N_CORE)
    for y in range(N_Y)
    for xh in range(N_XH)
]


def number(x, z, core, y, xh):
    return (((x * N_Z + z % N_Z) * N_CORE + core) * N_Y + y) * N_XH + xh


def routes(move):
    return [(number(*place), number(*move(*place))) for place in PLACES]


CELL_ROUNDS = (
    routes(lambda x, z, core, y, xh: (1 - x, z, core, y, 1 - xh)),
    routes(lambda x, z, core, y, xh: (x, z, core, y ^ 1, xh)),
    routes(lambda x, z, core, y, xh: (x, z, core, N_Y - 1 - y, xh)),
)
SWAP_X = routes(lambda x, z, core, y, xh: (1 - x, z, core, y, xh))
SWAP_CORE = routes(lambda x, z, core, y, xh: (x, z, 1 - core, y, xh))
RING_A = routes(lambda x, z, core, y, xh: (x, z + 1 - 2 * core, core, y, xh))
RING_B = routes(lambda x, z, core, y, xh: (x, z - 1 + 2 * core, core, y, xh))


def send(value, route):
    return lax.ppermute(value, AXES, route)


def score_blocks(blocks, groups, stores, out):
    n_rows, width = stores.shape
    step_rows = 512
    steps = n_rows // step_rows
    arrays = list({id(block[3]): block[3] for block in blocks}.values())
    number_of = {id(array): at for at, array in enumerate(arrays)}

    def body(*refs):
        array_refs = refs[: len(arrays)]
        store_ref = refs[len(arrays)]
        loads = []
        if out is None:
            out_ref, held_ref, rows_ref, acc_ref, sems, load_sems = refs[-6:]
            for step in range(steps):
                rows = pl.ds(step * step_rows, step_rows)
                load = pltpu.make_async_copy(store_ref.at[rows], held_ref.at[rows], load_sems.at[step])
                load.start()
                loads.append(load)
            store_ref = held_ref
        else:
            out_ref, rows_ref, acc_ref, sems = refs[-4:]
        tok, cell = lax.axis_index("tok"), lax.axis_index("cell")
        core = lax.rem(tok, N_CORE)
        z = lax.rem(lax.div(tok, N_CORE), N_Z)
        x = lax.rem(lax.div(tok, N_CORE * N_Z) + lax.rem(cell, N_XH), N_X)
        up = 1 - 2 * core

        def z_of(distance):
            return lax.rem(z + distance * up + N_Z, N_Z)

        starts = {}
        first = 0
        for group in groups:
            for at in group:
                _, own_x, distance, _, _ = blocks[at]
                x_at = x if own_x else 1 - x
                whole = len(group) > N_X
                place = x_at * N_Z + z_of(distance) if whole else x_at
                starts[at] = first + place * BLOCK
            first += len(group) * BLOCK
        for at, (_, _, _, array, index) in enumerate(blocks):
            start = pl.multiple_of(starts[at], BLOCK)
            rows_ref[pl.ds(start, BLOCK), :] = array_refs[number_of[id(array)]][index]
        copies = []
        for step in range(steps):
            cols = pl.ds(step * step_rows, step_rows)
            if loads:
                loads[step].wait()
            acc = lax.dot_general(
                rows_ref[...], store_ref[cols, :], NT, preferred_element_type=jnp.float32
            )
            acc_ref[:, :, cols] = acc.reshape(len(blocks), BLOCK, step_rows)
            first = 0
            for number_at, group in enumerate(groups):
                own_core, _, distance, _, _ = blocks[group[0]]
                core_at = core if own_core else 1 - core
                size = len(group) // N_X
                for x_at in range(N_X):
                    if size > 1:
                        source = acc_ref.at[pl.ds(first, size), :, cols]
                        target = out_ref.at[x_at, :, core_at, :, cols]
                    else:
                        source = acc_ref.at[first, :, cols]
                        target = out_ref.at[x_at, z_of(distance), core_at, :, cols]
                    first += size
                    copy = pltpu.make_async_copy(source, target, sems.at[step, number_at, x_at])
                    copy.start()
                    copies.append(copy)
        for copy in copies:
            copy.wait()

    vmem = pl.BlockSpec(memory_space=pltpu.VMEM)
    hbm = pl.BlockSpec(memory_space=pl.ANY)
    scores_shape = jax.ShapeDtypeStruct((N_X, N_Z, N_CORE, BLOCK, n_rows), jnp.float32)
    scratch = [
        pltpu.VMEM((len(blocks) * BLOCK, width), jnp.bfloat16),
        pltpu.VMEM((len(blocks), BLOCK, n_rows), jnp.float32),
        pltpu.SemaphoreType.DMA((steps, len(groups), N_X)),
    ]
    params = pltpu.CompilerParams(vmem_limit_bytes=12 << 20)
    if out is None:
        return pl.pallas_call(
            body,
            in_specs=[vmem] * len(arrays) + [pl.BlockSpec(memory_space=pltpu.HBM)],
            out_specs=(hbm, vmem),
            out_shape=(scores_shape, jax.ShapeDtypeStruct(stores.shape, stores.dtype)),
            scratch_shapes=[*scratch, pltpu.SemaphoreType.DMA((steps,))],
            compiler_params=params,
        )(*arrays, stores)
    return pl.pallas_call(
        body,
        in_specs=[vmem] * (len(arrays) + 1) + [hbm],
        out_specs=hbm,
        out_shape=scores_shape,
        scratch_shapes=scratch,
        compiler_params=params,
        input_output_aliases={len(arrays) + 1: 0},
    )(*arrays, stores, out)


def shards(activations, out_grads, query_ids, live, proj_in, proj_out, whitener, stores):
    tok_rows = activations.shape[0]
    valid_mask = (jnp.arange(tok_rows, dtype=jnp.int32) < live[0]).astype(jnp.float32)
    left_proj = jnp.dot(activations, proj_in, preferred_element_type=jnp.float32)
    right_proj = jnp.dot(out_grads, proj_out, preferred_element_type=jnp.float32)
    outer_cells = left_proj[:, :, None] * right_proj[:, None, :] * valid_mask[:, None, None]
    outer_cells = outer_cells.reshape(tok_rows, -1).astype(jnp.bfloat16)
    swap = (lax.axis_index("cell") % N_XH) * (Q // N_X)
    row_ids = jnp.arange(Q, dtype=jnp.int32) ^ swap
    onehot = (query_ids[:, None] == row_ids[None, :]).astype(jnp.bfloat16)
    partial_value = lax.dot_general(
        onehot, outer_cells, (((0,), (0,)), ((), ())), preferred_element_type=jnp.float32
    ).astype(jnp.bfloat16)
    pieces = lax.all_to_all(partial_value.reshape(N_TOK, BLOCK, -1), "tok", 0, 0, tiled=True)
    summed = pieces.astype(jnp.float32).sum(0).astype(jnp.bfloat16)
    total = jnp.dot(summed, whitener, preferred_element_type=jnp.float32)
    for route in CELL_ROUNDS:
        total = total + send(total.astype(jnp.bfloat16), route).astype(jnp.float32)
    own = total.astype(jnp.bfloat16)
    return gather_and_score(own, stores)


def gather_and_score(own, stores):
    here = (own, send(own, SWAP_X))
    up = tuple(send(piece, RING_A) for piece in here)
    down = tuple(send(piece, RING_B) for piece in here)
    far_own = send(up[0], RING_A)
    far_other = send(up[1], RING_A)
    near = jnp.stack([*here, *up, *down])
    near_over = send(near, SWAP_CORE)
    near_at = ((1, 0), (0, 0), (1, -1), (0, -1), (1, 1), (0, 1))
    blocks = [(1, own_x, distance, near, at) for at, (own_x, distance) in enumerate(near_at)]
    scores, held = score_blocks(blocks, ((0, 1), (2, 3), (4, 5)), stores, None)
    far = jnp.stack([far_own, far_other])
    far_over = send(far, SWAP_CORE)
    blocks = [(1, 1, 2, far, 0), (1, 0, 2, far, 1)]
    blocks += [(0, own_x, -distance, near_over, at) for at, (own_x, distance) in enumerate(near_at)]
    blocks += [(0, 1, 2, far_over, 0), (0, 0, 2, far_over, 1)]
    scores = score_blocks(blocks, ((0, 1), tuple(range(2, 10))), held, scores)
    return scores.reshape(Q, -1)


def solution(mesh):
    in_specs = (
        P("tok", None),
        P("tok", None),
        P("tok"),
        P("tok"),
        P(None, "cell"),
        P(),
        P("cell", None),
        P(("tok", "cell"), None),
    )
    out_specs = P(None, ("tok", "cell"))
    return jax.shard_map(shards, mesh=mesh, in_specs=in_specs, out_specs=out_specs, check_vma=False)
```

profile of v0, /device:TPU:1, one launch (start us, length us, event | category | flops | bytes accessed | tf_op | source)
XLA Modules:
  0.0 73.2 jit_solution(9351457334787515028)
XLA Ops:
  0.8 5.7 %fusion.7 = f32[1024,8]{0,1:T(8,128)S(1)} fusion(bf16[1024,4096]{1,0:T(8,128)(2,1)} %param.8, bf16[4096,8]{0,1:T(8,128)(2,1)} %param.12), kind=kOutput, calls=%fused_computation.23 | convolution fusion | flops 67108864 | bytes 8486912 | tf_op jit(solution)/shard_map/dot_general | solution.py:152
  6.5 0.7 fusion.8
  7.5 0.7 convolution_convert_fusion
  8.2 14.7 %all_to_all.5 = bf16[16,32,256]{2,1,0:T(8,128)(2,1)S(1)} all-to-all(bf16[16,32,256]{2,1,0:T(8,128)(2,1)S(1)} %bitcast.29), channel_id=1, replica_groups=mesh['tok'=16,'cell'=8] {'tok'}, dimensions={0} | all-to-all | bytes 524288 | tf_op jit(solution)/shard_map/all_to_all | solution.py:162
  23.0 0.3 fusion.6
  23.3 2.1 %collective-permute-start = (bf16[32,2048]{1,0:T(8,128)(2,1)S(1)}, bf16[32,2048]{1,0:T(8,128)(2,1)S(1)}, u32[]{:S(2)}, u32[]{:S(2)}) collective-permute-start(bf16[32,2048]{1,0:T(8,128)(2,1)S(1)} %get-tuple-element.11), channel_id=1, source_target_pairs={{0,65},{1,64},{2,67},{3,66},{4,69},{5,68},{6,71},{7,70},{8,73},{9,... | collective-permute-start | bytes 393224 | tf_op jit(solution)/shard_map/ppermute | solution.py:46
  25.4 3.3 %collective-permute-done = bf16[32,2048]{1,0:T(8,128)(2,1)S(1)} collective-permute-done((bf16[32,2048]{1,0:T(8,128)(2,1)S(1)}, bf16[32,2048]{1,0:T(8,128)(2,1)S(1)}, u32[]{:S(2)}, u32[]{:S(2)}) %collective-permute-start) | collective-permute-done | bytes 131104 | tf_op jit(solution)/shard_map/ppermute | solution.py:46
  28.7 1.4 %collective-permute-start.1 = (bf16[32,2048]{1,0:T(8,128)(2,1)S(1)}, bf16[32,2048]{1,0:T(8,128)(2,1)S(1)}, u32[]{:S(2)}, u32[]{:S(2)}) collective-permute-start(bf16[32,2048]{1,0:T(8,128)(2,1)S(1)} %fusion.3), channel_id=1, source_target_pairs={{0,2},{1,3},{2,0},{3,1},{4,6},{5,7},{6,4},{7,5},{8,10},{9,11},{10,... | collective-permute-start | bytes 393224 | tf_op jit(solution)/shard_map/ppermute | solution.py:46
  30.1 2.5 %collective-permute-done.1 = bf16[32,2048]{1,0:T(8,128)(2,1)S(1)} collective-permute-done((bf16[32,2048]{1,0:T(8,128)(2,1)S(1)}, bf16[32,2048]{1,0:T(8,128)(2,1)S(1)}, u32[]{:S(2)}, u32[]{:S(2)}) %collective-permute-start.1) | collective-permute-done | bytes 131104 | tf_op jit(solution)/shard_map/ppermute | solution.py:46
  32.7 2.8 %collective-permute-start.2 = (bf16[32,2048]{1,0:T(8,128)(2,1)S(1)}, bf16[32,2048]{1,0:T(8,128)(2,1)S(1)}, u32[]{:S(2)}, u32[]{:S(2)}) collective-permute-start(bf16[32,2048]{1,0:T(8,128)(2,1)S(1)} %fusion.4), channel_id=1, source_target_pairs={{0,6},{1,7},{2,4},{3,5},{4,2},{5,3},{6,0},{7,1},{8,14},{9,15},{10,... | collective-permute-start | bytes 393224 | tf_op jit(solution)/shard_map/ppermute | solution.py:46
  35.5 2.4 %collective-permute-done.2 = bf16[32,2048]{1,0:T(8,128)(2,1)S(1)} collective-permute-done((bf16[32,2048]{1,0:T(8,128)(2,1)S(1)}, bf16[32,2048]{1,0:T(8,128)(2,1)S(1)}, u32[]{:S(2)}, u32[]{:S(2)}) %collective-permute-start.2) | collective-permute-done | bytes 131104 | tf_op jit(solution)/shard_map/ppermute | solution.py:46
  38.0 2.3 %collective-permute-start.8 = (bf16[32,2048]{1,0:T(8,128)(2,1)S(1)}, bf16[32,2048]{1,0:T(8,128)(2,1)S(1)}, u32[]{:S(2)}, u32[]{:S(2)}) collective-permute-start(bf16[32,2048]{1,0:T(8,128)(2,1)S(1)} %get-tuple-element.10), channel_id=1, source_target_pairs={{0,48},{1,49},{2,50},{3,51},{4,52},{5,53},{6,54},{7,55},{8,24},{9,... | collective-permute-start | bytes 393224 | tf_op jit(solution)/shard_map/ppermute | solution.py:46
  40.3 0.5 collective-permute-start.3
  40.7 1.1 %collective-permute-done.5 = bf16[32,2048]{1,0:T(8,128)(2,1)S(1)} collective-permute-done((bf16[32,2048]{1,0:T(8,128)(2,1)S(1)}, bf16[32,2048]{1,0:T(8,128)(2,1)S(1)}, u32[]{:S(2)}, u32[]{:S(2)}) %collective-permute-start.5) | collective-permute-done | bytes 131104 | tf_op jit(solution)/shard_map/ppermute | solution.py:46
  41.8 2.2 %collective-permute-start.9 = (bf16[32,2048]{1,0:T(8,128)(2,1)S(1)}, bf16[32,2048]{1,0:T(8,128)(2,1)S(1)}, u32[]{:S(2)}, u32[]{:S(2)}) collective-permute-start(bf16[32,2048]{1,0:T(8,128)(2,1)S(1)} %collective-permute-done.5), channel_id=1, source_target_pairs={{0,48},{1,49},{2,50},{3,51},{4,52},{5,53},{6,54},{7,55},{8,24},{9,... | collective-permute-start | bytes 393224 | tf_op jit(solution)/shard_map/ppermute | solution.py:46
  44.0 0.5 collective-permute-start.6
  44.5 3.3 %collective-permute-done.6 = bf16[32,2048]{1,0:T(8,128)(2,1)S(1)} collective-permute-done((bf16[32,2048]{1,0:T(8,128)(2,1)S(1)}, bf16[32,2048]{1,0:T(8,128)(2,1)S(1)}, u32[]{:S(2)}, u32[]{:S(2)}) %collective-permute-start.6) | collective-permute-done | bytes 131104 | tf_op jit(solution)/shard_map/ppermute | solution.py:46
  47.9 7.1 %collective-permute-start.10 = (bf16[6,32,2048]{2,1,0:T(8,128)(2,1)S(1)}, bf16[6,32,2048]{2,1,0:T(8,128)(2,1)S(1)}, u32[]{:S(2)}, u32[]{:S(2)}) collective-permute-start(bf16[6,32,2048]{2,1,0:T(8,128)(2,1)S(1)} %bitcast_dynamic-update-slice_fusion.refs_0_), channel_id=1, source_target_pairs={{0,8},{1,9},{2,10},{3,11},{4,12},{5,13},{6,14},{7,15},{8,0},{9,1},... | collective-permute-start | bytes 2359304 | tf_op jit(solution)/shard_map/ppermute | solution.py:46
  55.1 3.7 %collective-permute-done.4 = bf16[32,2048]{1,0:T(8,128)(2,1)S(1)} collective-permute-done((bf16[32,2048]{1,0:T(8,128)(2,1)S(1)}, bf16[32,2048]{1,0:T(8,128)(2,1)S(1)}, u32[]{:S(2)}, u32[]{:S(2)}) %collective-permute-start.4) | collective-permute-done | bytes 131104 | tf_op jit(solution)/shard_map/ppermute | solution.py:46
  58.8 1.7 %collective-permute-done.7 = bf16[32,2048]{1,0:T(8,128)(2,1)S(1)} collective-permute-done((bf16[32,2048]{1,0:T(8,128)(2,1)S(1)}, bf16[32,2048]{1,0:T(8,128)(2,1)S(1)}, u32[]{:S(2)}, u32[]{:S(2)}) %collective-permute-start.7) | collective-permute-done | bytes 131104 | tf_op jit(solution)/shard_map/ppermute | solution.py:46
  60.5 2.2 %collective-permute-start.11 = (bf16[2,32,2048]{2,1,0:T(8,128)(2,1)S(1)}, bf16[2,32,2048]{2,1,0:T(8,128)(2,1)S(1)}, u32[]{:S(2)}, u32[]{:S(2)}) collective-permute-start(bf16[2,32,2048]{2,1,0:T(8,128)(2,1)S(1)} %pad_maximum_fusion.refs_0_), channel_id=1, source_target_pairs={{0,8},{1,9},{2,10},{3,11},{4,12},{5,13},{6,14},{7,15},{8,0},{9,1},... | collective-permute-start | bytes 786440 | tf_op jit(solution)/shard_map/ppermute | solution.py:46
  62.8 2.8 %copy-done.1 = bf16[1536,2048]{1,0:T(8,128)(2,1)S(1)} copy-done((bf16[1536,2048]{1,0:T(8,128)(2,1)S(1)}, bf16[1536,2048]{1,0:T(8,128)(2,1)}, u32[]{:S(2)}) %copy-start.1) | copy-done | bytes 6291480
  65.5 4.0 %shard_map.82 = (f32[2,4,2,32,1536]{4,3,2,1,0:T(8,128)}, bf16[1536,2048]{1,0:T(8,128)(2,1)S(1)}) custom-call(bf16[6,32,2048]{2,1,0:T(8,128)(2,1)S(1)} %bitcast_dynamic-update-slice_fusion.refs_0_, bf16[1536,2048]{1,0:T(8,128)(2,1)S(1)} %copy-done.1), custom_call_target="tpu_custom_call" | custom-call | tf_op jit(solution)/shard_map/pallas_call | solution.py:130
  69.5 3.6 %shard_map.83 = f32[2,4,2,32,1536]{4,3,2,1,0:T(8,128)} custom-call(bf16[2,32,2048]{2,1,0:T(8,128)(2,1)S(1)} %pad_maximum_fusion.refs_0_, bf16[6,32,2048]{2,1,0:T(8,128)(2,1)S(1)} %collective-permute-done.10.refs_1_, bf16[2,32,2048]{2,1,0:T(8,128)(2,1)S(1)} %collective-permute-done.11.refs_2_, ...), custom_call_target="tpu_custom_call", output_to_operand_aliasing={{}: (4, {})} | custom-call | tf_op jit(solution)/shard_map/pallas_call | solution.py:138
  (31 shorter events, 0.7 us)
Async XLA Ops:
  0.0 6.5 %copy-start = (bf16[1024,1024]{1,0:T(8,128)(2,1)S(1)}, bf16[1024,1024]{1,0:T(8,128)(2,1)}, u32[]{:S(2)}) copy-start(bf16[1024,1024]{1,0:T(8,128)(2,1)} %param.9) | copy-start | bytes 6291460
  0.8 5.7 %copy-start.3 = (bf16[1024,32]{0,1:T(8,128)(2,1)S(1)}, bf16[1024,32]{0,1:T(8,128)(2,1)}, u32[]{:S(2)}) copy-start(bf16[1024,32]{0,1:T(8,128)(2,1)} %param.13) | copy-start | bytes 196612
  6.5 1.0 %copy-start.4 = (s32[1024]{0:T(1024)S(1)}, s32[1024]{0:T(1024)}, u32[]{:S(2)}) copy-start(s32[1024]{0:T(1024)} %param.10) | copy-start | bytes 12292
  7.3 15.7 %copy-start.2 = (bf16[256,2048]{1,0:T(8,128)(2,1)S(1)}, bf16[256,2048]{1,0:T(8,128)(2,1)}, u32[]{:S(2)}) copy-start(bf16[256,2048]{1,0:T(8,128)(2,1)} %param.14) | copy-start | bytes 3145732
  23.3 5.4 %collective-permute-start = (bf16[32,2048]{1,0:T(8,128)(2,1)S(1)}, bf16[32,2048]{1,0:T(8,128)(2,1)S(1)}, u32[]{:S(2)}, u32[]{:S(2)}) collective-permute-start(bf16[32,2048]{1,0:T(8,128)(2,1)S(1)} %get-tuple-element.11), channel_id=1, source_target_pairs={{0,65},{1,64},{2,67},{3,66},{4,69},{5,68},{6,71},{7,70},{8,73},{9,... | collective-permute-start | bytes 393224 | tf_op jit(solution)/shard_map/ppermute | solution.py:46
  28.7 3.9 %collective-permute-start.1 = (bf16[32,2048]{1,0:T(8,128)(2,1)S(1)}, bf16[32,2048]{1,0:T(8,128)(2,1)S(1)}, u32[]{:S(2)}, u32[]{:S(2)}) collective-permute-start(bf16[32,2048]{1,0:T(8,128)(2,1)S(1)} %fusion.3), channel_id=1, source_target_pairs={{0,2},{1,3},{2,0},{3,1},{4,6},{5,7},{6,4},{7,5},{8,10},{9,11},{10,... | collective-permute-start | bytes 393224 | tf_op jit(solution)/shard_map/ppermute | solution.py:46
  32.7 5.2 %collective-permute-start.2 = (bf16[32,2048]{1,0:T(8,128)(2,1)S(1)}, bf16[32,2048]{1,0:T(8,128)(2,1)S(1)}, u32[]{:S(2)}, u32[]{:S(2)}) collective-permute-start(bf16[32,2048]{1,0:T(8,128)(2,1)S(1)} %fusion.4), channel_id=1, source_target_pairs={{0,6},{1,7},{2,4},{3,5},{4,2},{5,3},{6,0},{7,1},{8,14},{9,15},{10,... | collective-permute-start | bytes 393224 | tf_op jit(solution)/shard_map/ppermute | solution.py:46
  37.9 3.9 %collective-permute-start.5 = (bf16[32,2048]{1,0:T(8,128)(2,1)S(1)}, bf16[32,2048]{1,0:T(8,128)(2,1)S(1)}, u32[]{:S(2)}, u32[]{:S(2)}) collective-permute-start(bf16[32,2048]{1,0:T(8,128)(2,1)S(1)} %get-tuple-element.10), channel_id=1, source_target_pairs={{0,64},{1,65},{2,66},{3,67},{4,68},{5,69},{6,70},{7,71},{8,72},{9,... | collective-permute-start | bytes 393224 | tf_op jit(solution)/shard_map/ppermute | solution.py:46
  38.0 9.8 %collective-permute-start.8 = (bf16[32,2048]{1,0:T(8,128)(2,1)S(1)}, bf16[32,2048]{1,0:T(8,128)(2,1)S(1)}, u32[]{:S(2)}, u32[]{:S(2)}) collective-permute-start(bf16[32,2048]{1,0:T(8,128)(2,1)S(1)} %get-tuple-element.10), channel_id=1, source_target_pairs={{0,48},{1,49},{2,50},{3,51},{4,52},{5,53},{6,54},{7,55},{8,24},{9,... | collective-permute-start | bytes 393224 | tf_op jit(solution)/shard_map/ppermute | solution.py:46
  40.3 4.2 %collective-permute-start.3 = (bf16[32,2048]{1,0:T(8,128)(2,1)S(1)}, bf16[32,2048]{1,0:T(8,128)(2,1)S(1)}, u32[]{:S(2)}, u32[]{:S(2)}) collective-permute-start(bf16[32,2048]{1,0:T(8,128)(2,1)S(1)} %get-tuple-element.10), channel_id=1, source_target_pairs={{0,16},{1,17},{2,18},{3,19},{4,20},{5,21},{6,22},{7,23},{8,56},{9,... | collective-permute-start | bytes 393224 | tf_op jit(solution)/shard_map/ppermute | solution.py:46
  41.8 6.1 %collective-permute-start.9 = (bf16[32,2048]{1,0:T(8,128)(2,1)S(1)}, bf16[32,2048]{1,0:T(8,128)(2,1)S(1)}, u32[]{:S(2)}, u32[]{:S(2)}) collective-permute-start(bf16[32,2048]{1,0:T(8,128)(2,1)S(1)} %collective-permute-done.5), channel_id=1, source_target_pairs={{0,48},{1,49},{2,50},{3,51},{4,52},{5,53},{6,54},{7,55},{8,24},{9,... | collective-permute-start | bytes 393224 | tf_op jit(solution)/shard_map/ppermute | solution.py:46
  44.0 3.8 %collective-permute-start.6 = (bf16[32,2048]{1,0:T(8,128)(2,1)S(1)}, bf16[32,2048]{1,0:T(8,128)(2,1)S(1)}, u32[]{:S(2)}, u32[]{:S(2)}) collective-permute-start(bf16[32,2048]{1,0:T(8,128)(2,1)S(1)} %collective-permute-done.5), channel_id=1, source_target_pairs={{0,16},{1,17},{2,18},{3,19},{4,20},{5,21},{6,22},{7,23},{8,56},{9,... | collective-permute-start | bytes 393224 | tf_op jit(solution)/shard_map/ppermute | solution.py:46
  47.9 21.6 %collective-permute-start.10 = (bf16[6,32,2048]{2,1,0:T(8,128)(2,1)S(1)}, bf16[6,32,2048]{2,1,0:T(8,128)(2,1)S(1)}, u32[]{:S(2)}, u32[]{:S(2)}) collective-permute-start(bf16[6,32,2048]{2,1,0:T(8,128)(2,1)S(1)} %bitcast_dynamic-update-slice_fusion.refs_0_), channel_id=1, source_target_pairs={{0,8},{1,9},{2,10},{3,11},{4,12},{5,13},{6,14},{7,15},{8,0},{9,1},... | collective-permute-start | bytes 2359304 | tf_op jit(solution)/shard_map/ppermute | solution.py:46
  55.0 3.8 %collective-permute-start.4 = (bf16[32,2048]{1,0:T(8,128)(2,1)S(1)}, bf16[32,2048]{1,0:T(8,128)(2,1)S(1)}, u32[]{:S(2)}, u32[]{:S(2)}) collective-permute-start(bf16[32,2048]{1,0:T(8,128)(2,1)S(1)} %collective-permute-done.3), channel_id=1, source_target_pairs={{0,16},{1,17},{2,18},{3,19},{4,20},{5,21},{6,22},{7,23},{8,56},{9,... | collective-permute-start | bytes 393224 | tf_op jit(solution)/shard_map/ppermute | solution.py:46
  55.0 5.5 %collective-permute-start.7 = (bf16[32,2048]{1,0:T(8,128)(2,1)S(1)}, bf16[32,2048]{1,0:T(8,128)(2,1)S(1)}, u32[]{:S(2)}, u32[]{:S(2)}) collective-permute-start(bf16[32,2048]{1,0:T(8,128)(2,1)S(1)} %collective-permute-done.6), channel_id=1, source_target_pairs={{0,16},{1,17},{2,18},{3,19},{4,20},{5,21},{6,22},{7,23},{8,56},{9,... | collective-permute-start | bytes 393224 | tf_op jit(solution)/shard_map/ppermute | solution.py:46
  60.5 9.0 %collective-permute-start.11 = (bf16[2,32,2048]{2,1,0:T(8,128)(2,1)S(1)}, bf16[2,32,2048]{2,1,0:T(8,128)(2,1)S(1)}, u32[]{:S(2)}, u32[]{:S(2)}) collective-permute-start(bf16[2,32,2048]{2,1,0:T(8,128)(2,1)S(1)} %pad_maximum_fusion.refs_0_), channel_id=1, source_target_pairs={{0,8},{1,9},{2,10},{3,11},{4,12},{5,13},{6,14},{7,15},{8,0},{9,1},... | collective-permute-start | bytes 786440 | tf_op jit(solution)/shard_map/ppermute | solution.py:46
  62.8 2.8 %copy-start.1 = (bf16[1536,2048]{1,0:T(8,128)(2,1)S(1)}, bf16[1536,2048]{1,0:T(8,128)(2,1)}, u32[]{:S(2)}) copy-start(bf16[1536,2048]{1,0:T(8,128)(2,1)} %refs_1_.1) | copy-start | bytes 18874372
where the time goes:
time: 73.4 us; the launch traced here: 73.2 us
  starting transfers between devices  21.2 us (29%)
  waiting for transfers between devices  18 us (25%)
  blocking collectives  14.7 us (20%)
  Pallas kernels  7.6 us (10%)
  matrix products  7.36 us (10%)
  local copies, waits for them, and re-layouts  2.87 us (4%)
  between operations  1 us (1%)
    ppermute x12, starting transfers between devices, send(): return lax.ppermute(value, AXES, route)  21.2 us
    ppermute x12, waiting for transfers between devices, send(): return lax.ppermute(value, AXES, route)  18 us
    all_to_all x1, blocking collectives, shards(): lax.all_to_all(partial_value.reshape(N_TOK, BLOCK, -1), 'tok', 0, 0, tile...  14.7 us
    dot_general x1, matrix products, shards(): jnp.dot(activations, proj_in, preferred_element_type=jnp.float32)  5.67 us
    pallas_call x1, Pallas kernels, score_blocks(): pl.pallas_call(body, in_specs=[vmem] * len(arrays) + [pl.BlockSpec(memory...  3.96 us
    pallas_call x1, Pallas kernels, score_blocks(): pl.pallas_call(body, in_specs=[vmem] * (len(arrays) + 1) + [hbm], out_spe...  3.64 us
    unnamed x14, local copies, waits for them, and re-layouts  2.86 us
  transfers between devices with their start and end apart: 12, of which 7 were waited for; matrix products, arithmetic and copies ran while one was open for 0% of the time, Pallas kernels for 5%

commit v1 on v0

--- a/solution.py
+++ b/solution.py
@@ -31,11 +31,10 @@
     return [(number(*place), number(*move(*place))) for place in PLACES]
 
 
-CELL_ROUNDS = (
-    routes(lambda x, z, core, y, xh: (1 - x, z, core, y, 1 - xh)),
-    routes(lambda x, z, core, y, xh: (x, z, core, y ^ 1, xh)),
-    routes(lambda x, z, core, y, xh: (x, z, core, N_Y - 1 - y, xh)),
-)
+SUM_X = routes(lambda x, z, core, y, xh: (1 - x, z, core, y, 1 - xh))
+SUM_Y = [
+    routes(lambda x, z, core, y, xh, step=step: (x, z, core, (y + step * (1 - 2 * core)) % N_Y, xh)) for step in (1, 3, 2)
+]
 SWAP_X = routes(lambda x, z, core, y, xh: (1 - x, z, core, y, xh))
 SWAP_CORE = routes(lambda x, z, core, y, xh: (x, z, 1 - core, y, xh))
 RING_A = routes(lambda x, z, core, y, xh: (x, z + 1 - 2 * core, core, y, xh))
@@ -56,17 +55,7 @@
     def body(*refs):
         array_refs = refs[: len(arrays)]
         store_ref = refs[len(arrays)]
-        loads = []
-        if out is None:
-            out_ref, held_ref, rows_ref, acc_ref, sems, load_sems = refs[-6:]
-            for step in range(steps):
-                rows = pl.ds(step * step_rows, step_rows)
-                load = pltpu.make_async_copy(store_ref.at[rows], held_ref.at[rows], load_sems.at[step])
-                load.start()
-                loads.append(load)
-            store_ref = held_ref
-        else:
-            out_ref, rows_ref, acc_ref, sems = refs[-4:]
+        out_ref, rows_ref, acc_ref, sems = refs[-4:]
         tok, cell = lax.axis_index("tok"), lax.axis_index("cell")
         core = lax.rem(tok, N_CORE)
         z = lax.rem(lax.div(tok, N_CORE), N_Z)
@@ -92,8 +81,6 @@
         copies = []
         for step in range(steps):
             cols = pl.ds(step * step_rows, step_rows)
-            if loads:
-                loads[step].wait()
             acc = lax.dot_general(
                 rows_ref[...], store_ref[cols, :], NT, preferred_element_type=jnp.float32
             )
@@ -126,24 +113,43 @@
         pltpu.SemaphoreType.DMA((steps, len(groups), N_X)),
     ]
     params = pltpu.CompilerParams(vmem_limit_bytes=12 << 20)
-    if out is None:
-        return pl.pallas_call(
-            body,
-            in_specs=[vmem] * len(arrays) + [pl.BlockSpec(memory_space=pltpu.HBM)],
-            out_specs=(hbm, vmem),
-            out_shape=(scores_shape, jax.ShapeDtypeStruct(stores.shape, stores.dtype)),
-            scratch_shapes=[*scratch, pltpu.SemaphoreType.DMA((steps,))],
-            compiler_params=params,
-        )(*arrays, stores)
+    args = [*arrays, stores]
+    specs = [vmem] * len(args)
+    if out is not None:
+        args.append(out)
+        specs.append(hbm)
     return pl.pallas_call(
         body,
-        in_specs=[vmem] * (len(arrays) + 1) + [hbm],
+        in_specs=specs,
         out_specs=hbm,
         out_shape=scores_shape,
         scratch_shapes=scratch,
         compiler_params=params,
-        input_output_aliases={len(arrays) + 1: 0},
-    )(*arrays, stores, out)
+        input_output_aliases={} if out is None else {len(args) - 1: 0},
+    )(*args)
+
+
+def hold(stores):
+    parts = 4
+    size = stores.shape[0] // parts
+
+    def body(store_ref, held_ref, sems):
+        copies = []
+        for part in range(parts):
+            rows = pl.ds(part * size, size)
+            copies.append(pltpu.make_async_copy(store_ref.at[rows], held_ref.at[rows], sems.at[part]))
+            copies[-1].start()
+        for copy in copies:
+            copy.wait()
+
+    return pl.pallas_call(
+        body,
+        in_specs=[pl.BlockSpec(memory_space=pl.ANY)],
+        out_specs=pl.BlockSpec(memory_space=pltpu.VMEM),
+        out_shape=jax.ShapeDtypeStruct(stores.shape, stores.dtype),
+        scratch_shapes=[pltpu.SemaphoreType.DMA((parts,))],
+        compiler_params=pltpu.CompilerParams(vmem_limit_bytes=4 << 20),
+    )(pltpu.with_memory_space_constraint(stores, pltpu.HBM))
 
 
 def shards(activations, out_grads, query_ids, live, proj_in, proj_out, whitener, stores):
@@ -162,13 +168,16 @@
     pieces = lax.all_to_all(partial_value.reshape(N_TOK, BLOCK, -1), "tok", 0, 0, tiled=True)
     summed = pieces.astype(jnp.float32).sum(0).astype(jnp.bfloat16)
     total = jnp.dot(summed, whitener, preferred_element_type=jnp.float32)
-    for route in CELL_ROUNDS:
-        total = total + send(total.astype(jnp.bfloat16), route).astype(jnp.float32)
-    own = total.astype(jnp.bfloat16)
-    return gather_and_score(own, stores)
-
-
-def gather_and_score(own, stores):
+    across = send(total.astype(jnp.bfloat16), SUM_X)
+    held = hold(stores)
+    total = total + across.astype(jnp.float32)
+    rounded = total.astype(jnp.bfloat16)
+    for piece in [send(rounded, route) for route in SUM_Y]:
+        total = total + piece.astype(jnp.float32)
+    return gather_and_score(total.astype(jnp.bfloat16), held)
+
+
+def gather_and_score(own, held):
     here = (own, send(own, SWAP_X))
     up = tuple(send(piece, RING_A) for piece in here)
     down = tuple(send(piece, RING_B) for piece in here)
@@ -178,7 +187,7 @@
     near_over = send(near, SWAP_CORE)
     near_at = ((1, 0), (0, 0), (1, -1), (0, -1), (1, 1), (0, 1))
     blocks = [(1, own_x, distance, near, at) for at, (own_x, distance) in enumerate(near_at)]
-    scores, held = score_blocks(blocks, ((0, 1), (2, 3), (4, 5)), stores, None)
+    scores = score_blocks(blocks, ((0, 1), (2, 3), (4, 5)), held, None)
     far = jnp.stack([far_own, far_other])
     far_over = send(far, SWAP_CORE)
     blocks = [(1, 1, 2, far, 0), (1, 0, 2, far, 1)]

time: 73.4 us -> 71.7 us (0.977)
  local copies, waits for them, and re-layouts: 2.87 us -> 0.08 us
  Pallas kernels: 7.6 us -> 9.61 us
    unnamed x14 -> x12, local copies, waits for them, and re-layouts: 2.86 us -> 0.07 us
    pallas_call x2 -> x3, Pallas kernels: 7.6 us -> 9.61 us  [the longest x2 6.75 us: score_blocks(): pl.pallas_call(body, in_specs=specs, out_specs=hbm, out_shape=scores_shap...]
    ppermute x12 -> x13, waiting for transfers between devices: 18 us -> 17.3 us  [send(): return lax.ppermute(value, AXES, route)]
    ppermute x12 -> x13, starting transfers between devices: 21.2 us -> 21.1 us  [send(): return lax.ppermute(value, AXES, route)]
  transfers between devices with their start and end apart: 12 -> 13, of which waited for: 7 -> 8; matrix products, arithmetic and copies ran while one was open for 0% -> 0% of each run, Pallas kernels for 5% -> 8%
where the time goes in v1:
time: 71.7 us; the launch traced here: 71.6 us
  starting transfers between devices  21.1 us (29%)
  waiting for transfers between devices  17.3 us (24%)
  blocking collectives  14.7 us (21%)
  Pallas kernels  9.61 us (13%)
  matrix products  7.36 us (10%)
  between operations  0.99 us (1%)
    ppermute x13, starting transfers between devices, send(): return lax.ppermute(value, AXES, route)  21.1 us
    ppermute x13, waiting for transfers between devices, send(): return lax.ppermute(value, AXES, route)  17.3 us
    all_to_all x1, blocking collectives, shards(): lax.all_to_all(partial_value.reshape(N_TOK, BLOCK, -1), 'tok', 0, 0, tile...  14.7 us
    pallas_call x2, Pallas kernels, score_blocks(): pl.pallas_call(body, in_specs=specs, out_specs=hbm, out_shape=scores_shap...  6.75 us
    dot_general x1, matrix products, shards(): jnp.dot(activations, proj_in, preferred_element_type=jnp.float32)  5.67 us
    pallas_call x1, Pallas kernels, hold(): pl.pallas_call(body, in_specs=[pl.BlockSpec(memory_space=pl.ANY)], out_sp...  2.87 us
  transfers between devices with their start and end apart: 13, of which 8 were waited for; matrix products, arithmetic and copies ran while one was open for 0% of the time, Pallas kernels for 8%

profile of v1, /device:TPU:1, one launch (start us, length us, event | category | flops | bytes accessed | tf_op | source)
XLA Modules:
  0.0 71.6 jit_solution(7705341882949329434)
XLA Ops:
  0.8 5.7 %fusion.6 = f32[1024,8]{0,1:T(8,128)S(1)} fusion(bf16[1024,4096]{1,0:T(8,128)(2,1)} %param.8, bf16[4096,8]{0,1:T(8,128)(2,1)} %param.12), kind=kOutput, calls=%fused_computation.21 | convolution fusion | flops 67108864 | bytes 8486912 | tf_op jit(solution)/shard_map/dot_general | solution.py:158
  6.5 0.7 fusion.7
  7.5 0.7 convolution_convert_fusion
  8.2 14.7 %all_to_all.5 = bf16[16,32,256]{2,1,0:T(8,128)(2,1)S(1)} all-to-all(bf16[16,32,256]{2,1,0:T(8,128)(2,1)S(1)} %bitcast.29), channel_id=1, replica_groups=mesh['tok'=16,'cell'=8] {'tok'}, dimensions={0} | all-to-all | bytes 524288 | tf_op jit(solution)/shard_map/all_to_all | solution.py:168
  23.3 2.1 %collective-permute-start = (bf16[32,2048]{1,0:T(8,128)(2,1)S(1)}, bf16[32,2048]{1,0:T(8,128)(2,1)S(1)}, u32[]{:S(2)}, u32[]{:S(2)}) collective-permute-start(bf16[32,2048]{1,0:T(8,128)(2,1)S(1)} %get-tuple-element.7), channel_id=1, source_target_pairs={{0,65},{1,64},{2,67},{3,66},{4,69},{5,68},{6,71},{7,70},{8,73},{9,... | collective-permute-start | bytes 393224 | tf_op jit(solution)/shard_map/ppermute | solution.py:45
  25.4 3.3 %collective-permute-done = bf16[32,2048]{1,0:T(8,128)(2,1)S(1)} collective-permute-done((bf16[32,2048]{1,0:T(8,128)(2,1)S(1)}, bf16[32,2048]{1,0:T(8,128)(2,1)S(1)}, u32[]{:S(2)}, u32[]{:S(2)}) %collective-permute-start) | collective-permute-done | bytes 131104 | tf_op jit(solution)/shard_map/ppermute | solution.py:45
  28.7 3.0 %collective-permute-start.3 = (bf16[32,2048]{1,0:T(8,128)(2,1)S(1)}, bf16[32,2048]{1,0:T(8,128)(2,1)S(1)}, u32[]{:S(2)}, u32[]{:S(2)}) collective-permute-start(bf16[32,2048]{1,0:T(8,128)(2,1)S(1)} %fusion.3), channel_id=1, source_target_pairs={{0,4},{1,5},{2,6},{3,7},{4,0},{5,1},{6,2},{7,3},{8,12},{9,13},{10,... | collective-permute-start | bytes 393224 | tf_op jit(solution)/shard_map/ppermute | solution.py:45
  32.1 2.3 %collective-permute-start.1 = (bf16[32,2048]{1,0:T(8,128)(2,1)S(1)}, bf16[32,2048]{1,0:T(8,128)(2,1)S(1)}, u32[]{:S(2)}, u32[]{:S(2)}) collective-permute-start(bf16[32,2048]{1,0:T(8,128)(2,1)S(1)} %fusion.3), channel_id=1, source_target_pairs={{0,2},{1,3},{2,4},{3,5},{4,6},{5,7},{6,0},{7,1},{8,14},{9,15},{10,... | collective-permute-start | bytes 393224 | tf_op jit(solution)/shard_map/ppermute | solution.py:45
  34.4 3.6 %collective-permute-done.2 = bf16[32,2048]{1,0:T(8,128)(2,1)S(1)} collective-permute-done((bf16[32,2048]{1,0:T(8,128)(2,1)S(1)}, bf16[32,2048]{1,0:T(8,128)(2,1)S(1)}, u32[]{:S(2)}, u32[]{:S(2)}) %collective-permute-start.2) | collective-permute-done | bytes 131104 | tf_op jit(solution)/shard_map/ppermute | solution.py:45
  38.0 0.7 collective-permute-done.1
  38.8 1.0 %collective-permute-start.9 = (bf16[32,2048]{1,0:T(8,128)(2,1)S(1)}, bf16[32,2048]{1,0:T(8,128)(2,1)S(1)}, u32[]{:S(2)}, u32[]{:S(2)}) collective-permute-start(bf16[32,2048]{1,0:T(8,128)(2,1)S(1)} %get-tuple-element.6), channel_id=1, source_target_pairs={{0,48},{1,49},{2,50},{3,51},{4,52},{5,53},{6,54},{7,55},{8,24},{9,... | collective-permute-start | bytes 393224 | tf_op jit(solution)/shard_map/ppermute | solution.py:45
  39.8 1.8 %collective-permute-start.4 = (bf16[32,2048]{1,0:T(8,128)(2,1)S(1)}, bf16[32,2048]{1,0:T(8,128)(2,1)S(1)}, u32[]{:S(2)}, u32[]{:S(2)}) collective-permute-start(bf16[32,2048]{1,0:T(8,128)(2,1)S(1)} %get-tuple-element.6), channel_id=1, source_target_pairs={{0,16},{1,17},{2,18},{3,19},{4,20},{5,21},{6,22},{7,23},{8,56},{9,... | collective-permute-start | bytes 393224 | tf_op jit(solution)/shard_map/ppermute | solution.py:45
  41.6 1.1 %collective-permute-done.6 = bf16[32,2048]{1,0:T(8,128)(2,1)S(1)} collective-permute-done((bf16[32,2048]{1,0:T(8,128)(2,1)S(1)}, bf16[32,2048]{1,0:T(8,128)(2,1)S(1)}, u32[]{:S(2)}, u32[]{:S(2)}) %collective-permute-start.6) | collective-permute-done | bytes 131104 | tf_op jit(solution)/shard_map/ppermute | solution.py:45
  42.6 0.9 %collective-permute-start.10 = (bf16[32,2048]{1,0:T(8,128)(2,1)S(1)}, bf16[32,2048]{1,0:T(8,128)(2,1)S(1)}, u32[]{:S(2)}, u32[]{:S(2)}) collective-permute-start(bf16[32,2048]{1,0:T(8,128)(2,1)S(1)} %collective-permute-done.6), channel_id=1, source_target_pairs={{0,48},{1,49},{2,50},{3,51},{4,52},{5,53},{6,54},{7,55},{8,24},{9,... | collective-permute-start | bytes 393224 | tf_op jit(solution)/shard_map/ppermute | solution.py:45
  43.5 1.8 %collective-permute-start.7 = (bf16[32,2048]{1,0:T(8,128)(2,1)S(1)}, bf16[32,2048]{1,0:T(8,128)(2,1)S(1)}, u32[]{:S(2)}, u32[]{:S(2)}) collective-permute-start(bf16[32,2048]{1,0:T(8,128)(2,1)S(1)} %collective-permute-done.6), channel_id=1, source_target_pairs={{0,16},{1,17},{2,18},{3,19},{4,20},{5,21},{6,22},{7,23},{8,56},{9,... | collective-permute-start | bytes 393224 | tf_op jit(solution)/shard_map/ppermute | solution.py:45
  45.3 2.3 %collective-permute-done.7 = bf16[32,2048]{1,0:T(8,128)(2,1)S(1)} collective-permute-done((bf16[32,2048]{1,0:T(8,128)(2,1)S(1)}, bf16[32,2048]{1,0:T(8,128)(2,1)S(1)}, u32[]{:S(2)}, u32[]{:S(2)}) %collective-permute-start.7) | collective-permute-done | bytes 131104 | tf_op jit(solution)/shard_map/ppermute | solution.py:45
  47.7 0.9 %collective-permute-done.10 = bf16[32,2048]{1,0:T(8,128)(2,1)S(1)} collective-permute-done((bf16[32,2048]{1,0:T(8,128)(2,1)S(1)}, bf16[32,2048]{1,0:T(8,128)(2,1)S(1)}, u32[]{:S(2)}, u32[]{:S(2)}) %collective-permute-start.10) | collective-permute-done | bytes 131104 | tf_op jit(solution)/shard_map/ppermute | solution.py:45
  48.6 5.6 %collective-permute-start.11 = (bf16[6,32,2048]{2,1,0:T(8,128)(2,1)S(1)}, bf16[6,32,2048]{2,1,0:T(8,128)(2,1)S(1)}, u32[]{:S(2)}, u32[]{:S(2)}) collective-permute-start(bf16[6,32,2048]{2,1,0:T(8,128)(2,1)S(1)} %bitcast_dynamic-update-slice_fusion.refs_0_), channel_id=1, source_target_pairs={{0,8},{1,9},{2,10},{3,11},{4,12},{5,13},{6,14},{7,15},{8,0},{9,1},... | collective-permute-start | bytes 2359304 | tf_op jit(solution)/shard_map/ppermute | solution.py:45
  54.2 3.8 %collective-permute-done.5 = bf16[32,2048]{1,0:T(8,128)(2,1)S(1)} collective-permute-done((bf16[32,2048]{1,0:T(8,128)(2,1)S(1)}, bf16[32,2048]{1,0:T(8,128)(2,1)S(1)}, u32[]{:S(2)}, u32[]{:S(2)}) %collective-permute-start.5) | collective-permute-done | bytes 131104 | tf_op jit(solution)/shard_map/ppermute | solution.py:45
  58.0 1.7 %collective-permute-done.8 = bf16[32,2048]{1,0:T(8,128)(2,1)S(1)} collective-permute-done((bf16[32,2048]{1,0:T(8,128)(2,1)S(1)}, bf16[32,2048]{1,0:T(8,128)(2,1)S(1)}, u32[]{:S(2)}, u32[]{:S(2)}) %collective-permute-start.8) | collective-permute-done | bytes 131104 | tf_op jit(solution)/shard_map/ppermute | solution.py:45
  59.7 2.2 %collective-permute-start.12 = (bf16[2,32,2048]{2,1,0:T(8,128)(2,1)S(1)}, bf16[2,32,2048]{2,1,0:T(8,128)(2,1)S(1)}, u32[]{:S(2)}, u32[]{:S(2)}) collective-permute-start(bf16[2,32,2048]{2,1,0:T(8,128)(2,1)S(1)} %pad_maximum_fusion.refs_0_), channel_id=1, source_target_pairs={{0,8},{1,9},{2,10},{3,11},{4,12},{5,13},{6,14},{7,15},{8,0},{9,1},... | collective-permute-start | bytes 786440 | tf_op jit(solution)/shard_map/ppermute | solution.py:45
  61.9 2.9 %shard_map.82.refs_1_.refs_3_ = bf16[1536,2048]{1,0:T(8,128)(2,1)S(1)} custom-call(bf16[1536,2048]{1,0:T(8,128)(2,1)} %store_ref.1), custom_call_target="tpu_custom_call" | custom-call | tf_op jit(solution)/shard_map/pallas_call | solution.py:145
  64.8 3.1 %shard_map.83.refs_4_ = f32[2,4,2,32,1536]{4,3,2,1,0:T(8,128)} custom-call(bf16[6,32,2048]{2,1,0:T(8,128)(2,1)S(1)} %bitcast_dynamic-update-slice_fusion.refs_0_, bf16[1536,2048]{1,0:T(8,128)(2,1)S(1)} %shard_map.82.refs_1_.refs_3_), custom_call_target="tpu_custom_call" | custom-call | tf_op jit(solution)/shard_map/pallas_call | solution.py:121
  67.9 3.6 %shard_map.84 = f32[2,4,2,32,1536]{4,3,2,1,0:T(8,128)} custom-call(bf16[2,32,2048]{2,1,0:T(8,128)(2,1)S(1)} %pad_maximum_fusion.refs_0_, bf16[6,32,2048]{2,1,0:T(8,128)(2,1)S(1)} %collective-permute-done.11.refs_1_, bf16[2,32,2048]{2,1,0:T(8,128)(2,1)S(1)} %collective-permute-done.12.refs_2_, ...), custom_call_target="tpu_custom_call", output_to_operand_aliasing={{}: (4, {})} | custom-call | tf_op jit(solution)/shard_map/pallas_call | solution.py:121
  (31 shorter events, 1.3 us)
Async XLA Ops:
  0.0 6.5 %copy-start = (bf16[1024,1024]{1,0:T(8,128)(2,1)S(1)}, bf16[1024,1024]{1,0:T(8,128)(2,1)}, u32[]{:S(2)}) copy-start(bf16[1024,1024]{1,0:T(8,128)(2,1)} %param.9) | copy-start | bytes 6291460
  0.8 5.7 %copy-start.2 = (bf16[1024,32]{0,1:T(8,128)(2,1)S(1)}, bf16[1024,32]{0,1:T(8,128)(2,1)}, u32[]{:S(2)}) copy-start(bf16[1024,32]{0,1:T(8,128)(2,1)} %param.13) | copy-start | bytes 196612
  6.5 1.0 %copy-start.3 = (s32[1024]{0:T(1024)S(1)}, s32[1024]{0:T(1024)}, u32[]{:S(2)}) copy-start(s32[1024]{0:T(1024)} %param.10) | copy-start | bytes 12292
  7.3 15.7 %copy-start.1 = (bf16[256,2048]{1,0:T(8,128)(2,1)S(1)}, bf16[256,2048]{1,0:T(8,128)(2,1)}, u32[]{:S(2)}) copy-start(bf16[256,2048]{1,0:T(8,128)(2,1)} %param.14) | copy-start | bytes 3145732
  23.3 5.4 %collective-permute-start = (bf16[32,2048]{1,0:T(8,128)(2,1)S(1)}, bf16[32,2048]{1,0:T(8,128)(2,1)S(1)}, u32[]{:S(2)}, u32[]{:S(2)}) collective-permute-start(bf16[32,2048]{1,0:T(8,128)(2,1)S(1)} %get-tuple-element.7), channel_id=1, source_target_pairs={{0,65},{1,64},{2,67},{3,66},{4,69},{5,68},{6,71},{7,70},{8,73},{9,... | collective-permute-start | bytes 393224 | tf_op jit(solution)/shard_map/ppermute | solution.py:45
  28.7 5.7 %collective-permute-start.3 = (bf16[32,2048]{1,0:T(8,128)(2,1)S(1)}, bf16[32,2048]{1,0:T(8,128)(2,1)S(1)}, u32[]{:S(2)}, u32[]{:S(2)}) collective-permute-start(bf16[32,2048]{1,0:T(8,128)(2,1)S(1)} %fusion.3), channel_id=1, source_target_pairs={{0,4},{1,5},{2,6},{3,7},{4,0},{5,1},{6,2},{7,3},{8,12},{9,13},{10,... | collective-permute-start | bytes 393224 | tf_op jit(solution)/shard_map/ppermute | solution.py:45
  31.7 6.2 %collective-permute-start.2 = (bf16[32,2048]{1,0:T(8,128)(2,1)S(1)}, bf16[32,2048]{1,0:T(8,128)(2,1)S(1)}, u32[]{:S(2)}, u32[]{:S(2)}) collective-permute-start(bf16[32,2048]{1,0:T(8,128)(2,1)S(1)} %fusion.3), channel_id=1, source_target_pairs={{0,6},{1,7},{2,0},{3,1},{4,2},{5,3},{6,4},{7,5},{8,10},{9,11},{10,... | collective-permute-start | bytes 393224 | tf_op jit(solution)/shard_map/ppermute | solution.py:45
  32.1 6.5 %collective-permute-start.1 = (bf16[32,2048]{1,0:T(8,128)(2,1)S(1)}, bf16[32,2048]{1,0:T(8,128)(2,1)S(1)}, u32[]{:S(2)}, u32[]{:S(2)}) collective-permute-start(bf16[32,2048]{1,0:T(8,128)(2,1)S(1)} %fusion.3), channel_id=1, source_target_pairs={{0,2},{1,3},{2,4},{3,5},{4,6},{5,7},{6,0},{7,1},{8,14},{9,15},{10,... | collective-permute-start | bytes 393224 | tf_op jit(solution)/shard_map/ppermute | solution.py:45
  38.7 3.9 %collective-permute-start.6 = (bf16[32,2048]{1,0:T(8,128)(2,1)S(1)}, bf16[32,2048]{1,0:T(8,128)(2,1)S(1)}, u32[]{:S(2)}, u32[]{:S(2)}) collective-permute-start(bf16[32,2048]{1,0:T(8,128)(2,1)S(1)} %get-tuple-element.6), channel_id=1, source_target_pairs={{0,64},{1,65},{2,66},{3,67},{4,68},{5,69},{6,70},{7,71},{8,72},{9,... | collective-permute-start | bytes 393224 | tf_op jit(solution)/shard_map/ppermute | solution.py:45
  38.8 8.8 %collective-permute-start.9 = (bf16[32,2048]{1,0:T(8,128)(2,1)S(1)}, bf16[32,2048]{1,0:T(8,128)(2,1)S(1)}, u32[]{:S(2)}, u32[]{:S(2)}) collective-permute-start(bf16[32,2048]{1,0:T(8,128)(2,1)S(1)} %get-tuple-element.6), channel_id=1, source_target_pairs={{0,48},{1,49},{2,50},{3,51},{4,52},{5,53},{6,54},{7,55},{8,24},{9,... | collective-permute-start | bytes 393224 | tf_op jit(solution)/shard_map/ppermute | solution.py:45
  39.8 5.5 %collective-permute-start.4 = (bf16[32,2048]{1,0:T(8,128)(2,1)S(1)}, bf16[32,2048]{1,0:T(8,128)(2,1)S(1)}, u32[]{:S(2)}, u32[]{:S(2)}) collective-permute-start(bf16[32,2048]{1,0:T(8,128)(2,1)S(1)} %get-tuple-element.6), channel_id=1, source_target_pairs={{0,16},{1,17},{2,18},{3,19},{4,20},{5,21},{6,22},{7,23},{8,56},{9,... | collective-permute-start | bytes 393224 | tf_op jit(solution)/shard_map/ppermute | solution.py:45
  42.6 5.9 %collective-permute-start.10 = (bf16[32,2048]{1,0:T(8,128)(2,1)S(1)}, bf16[32,2048]{1,0:T(8,128)(2,1)S(1)}, u32[]{:S(2)}, u32[]{:S(2)}) collective-permute-start(bf16[32,2048]{1,0:T(8,128)(2,1)S(1)} %collective-permute-done.6), channel_id=1, source_target_pairs={{0,48},{1,49},{2,50},{3,51},{4,52},{5,53},{6,54},{7,55},{8,24},{9,... | collective-permute-start | bytes 393224 | tf_op jit(solution)/shard_map/ppermute | solution.py:45
  43.5 4.1 %collective-permute-start.7 = (bf16[32,2048]{1,0:T(8,128)(2,1)S(1)}, bf16[32,2048]{1,0:T(8,128)(2,1)S(1)}, u32[]{:S(2)}, u32[]{:S(2)}) collective-permute-start(bf16[32,2048]{1,0:T(8,128)(2,1)S(1)} %collective-permute-done.6), channel_id=1, source_target_pairs={{0,16},{1,17},{2,18},{3,19},{4,20},{5,21},{6,22},{7,23},{8,56},{9,... | collective-permute-start | bytes 393224 | tf_op jit(solution)/shard_map/ppermute | solution.py:45
  48.6 19.4 %collective-permute-start.11 = (bf16[6,32,2048]{2,1,0:T(8,128)(2,1)S(1)}, bf16[6,32,2048]{2,1,0:T(8,128)(2,1)S(1)}, u32[]{:S(2)}, u32[]{:S(2)}) collective-permute-start(bf16[6,32,2048]{2,1,0:T(8,128)(2,1)S(1)} %bitcast_dynamic-update-slice_fusion.refs_0_), channel_id=1, source_target_pairs={{0,8},{1,9},{2,10},{3,11},{4,12},{5,13},{6,14},{7,15},{8,0},{9,1},... | collective-permute-start | bytes 2359304 | tf_op jit(solution)/shard_map/ppermute | solution.py:45
  54.2 3.8 %collective-permute-start.5 = (bf16[32,2048]{1,0:T(8,128)(2,1)S(1)}, bf16[32,2048]{1,0:T(8,128)(2,1)S(1)}, u32[]{:S(2)}, u32[]{:S(2)}) collective-permute-start(bf16[32,2048]{1,0:T(8,128)(2,1)S(1)} %collective-permute-done.4), channel_id=1, source_target_pairs={{0,16},{1,17},{2,18},{3,19},{4,20},{5,21},{6,22},{7,23},{8,56},{9,... | collective-permute-start | bytes 393224 | tf_op jit(solution)/shard_map/ppermute | solution.py:45
  54.2 5.5 %collective-permute-start.8 = (bf16[32,2048]{1,0:T(8,128)(2,1)S(1)}, bf16[32,2048]{1,0:T(8,128)(2,1)S(1)}, u32[]{:S(2)}, u32[]{:S(2)}) collective-permute-start(bf16[32,2048]{1,0:T(8,128)(2,1)S(1)} %collective-permute-done.7), channel_id=1, source_target_pairs={{0,16},{1,17},{2,18},{3,19},{4,20},{5,21},{6,22},{7,23},{8,56},{9,... | collective-permute-start | bytes 393224 | tf_op jit(solution)/shard_map/ppermute | solution.py:45
  59.7 8.2 %collective-permute-start.12 = (bf16[2,32,2048]{2,1,0:T(8,128)(2,1)S(1)}, bf16[2,32,2048]{2,1,0:T(8,128)(2,1)S(1)}, u32[]{:S(2)}, u32[]{:S(2)}) collective-permute-start(bf16[2,32,2048]{2,1,0:T(8,128)(2,1)S(1)} %pad_maximum_fusion.refs_0_), channel_id=1, source_target_pairs={{0,8},{1,9},{2,10},{3,11},{4,12},{5,13},{6,14},{7,15},{8,0},{9,1},... | collective-permute-start | bytes 786440 | tf_op jit(solution)/shard_map/ppermute | solution.py:45

commit v2 on v1

v2 whole, which is shorter than its diff:
```python
import jax
import jax.numpy as jnp
from jax import lax
from jax.experimental import pallas as pl
from jax.experimental.pallas import tpu as pltpu
from jax.sharding import PartitionSpec as P

Q = 512
N_X, N_Z, N_CORE, N_Y, N_XH = 2, 4, 2, 4, 2
N_TOK = N_X * N_Z * N_CORE
BLOCK = Q // N_TOK
AXES = ("tok", "cell")
NT = (((1,), (1,)), ((), ()))
STEP_ROWS = 512


PLACES = [
    (x, z, core, y, xh)
    for x in range(N_X)
    for z in range(N_Z)
    for core in range(N_CORE)
    for y in range(N_Y)
    for xh in range(N_XH)
]


def number(x, z, core, y, xh):
    return (((x * N_Z + z % N_Z) * N_CORE + core) * N_Y + y) * N_XH + xh


def routes(move):
    return [(number(*place), number(*move(*place))) for place in PLACES]


SUM_X = routes(lambda x, z, core, y, xh: (1 - x, z, core, y, 1 - xh))
SUM_Y = [
    routes(lambda x, z, core, y, xh, step=step: (x, z, core, (y + step * (1 - 2 * core)) % N_Y, xh)) for step in (1, 3, 2)
]
SWAP_X = routes(lambda x, z, core, y, xh: (1 - x, z, core, y, xh))
SWAP_CORE = routes(lambda x, z, core, y, xh: (x, z, 1 - core, y, xh))
RING_A = routes(lambda x, z, core, y, xh: (x, z + 1 - 2 * core, core, y, xh))
RING_B = routes(lambda x, z, core, y, xh: (x, z - 1 + 2 * core, core, y, xh))


def send(value, route):
    return lax.ppermute(value, AXES, route)


NEAR_BLOCKS = ((0, 0), (1, 0), (0, -1), (1, -1), (0, 1), (1, 1))
N_NEAR = 3


def place():
    tok, cell = lax.axis_index("tok"), lax.axis_index("cell")
    core = lax.rem(tok, N_CORE)
    z = lax.rem(lax.div(tok, N_CORE), N_Z)
    x = lax.rem(lax.div(tok, N_CORE * N_Z) + lax.rem(cell, N_XH), N_X)

    def z_of(distance):
        return lax.rem(z + distance * (1 - 2 * core) + N_Z, N_Z)

    return x, z_of, core


def block_at(number):
    return pl.ds(pl.multiple_of(number * BLOCK, BLOCK), BLOCK)


def score_near(near, held):
    n_rows, width = held.shape

    def body(near_ref, store_ref, out_ref, rows_ref):
        x, _, _ = place()
        for at, (turn, _) in enumerate(NEAR_BLOCKS):
            x_at = 1 - x if turn else x
            rows_ref[block_at(at // N_X * N_X + x_at), :] = near_ref[at]
        for step in range(n_rows // STEP_ROWS):
            cols = pl.ds(step * STEP_ROWS, STEP_ROWS)
            scores = lax.dot_general(
                rows_ref[...], store_ref[cols, :], NT, preferred_element_type=jnp.float32
            )
            out_ref[:, :, :, cols] = scores.reshape(N_NEAR, N_X, BLOCK, STEP_ROWS)

    vmem = pl.BlockSpec(memory_space=pltpu.VMEM)
    return pl.pallas_call(
        body,
        in_specs=[vmem, vmem],
        out_specs=vmem,
        out_shape=jax.ShapeDtypeStruct((N_NEAR, N_X, BLOCK, n_rows), jnp.float32),
        scratch_shapes=[pltpu.VMEM((len(NEAR_BLOCKS) * BLOCK, width), jnp.bfloat16)],
        compiler_params=pltpu.CompilerParams(vmem_limit_bytes=8 << 20),
    )(near, held)


def score_rest(near_scores, far, near_over, far_over, held):
    n_rows, width = held.shape
    steps = n_rows // STEP_ROWS

    def body(
        near_scores_ref, far_ref, near_over_ref, far_over_ref, store_ref, out_ref,
        rows_ref, far_acc_ref, over_acc_ref, near_sems, sems,
    ):
        x, z_of, core = place()
        copies = []
        for at in range(N_NEAR):
            distance = NEAR_BLOCKS[at * N_X][1]
            copies.append(
                pltpu.make_async_copy(near_scores_ref.at[at], out_ref.at[:, z_of(distance), core], near_sems.at[at])
            )
            copies[-1].start()
        for turn in range(N_X):
            x_at = 1 - x if turn else x
            rows_ref[block_at(x_at), :] = far_ref[turn]
            rows_ref[block_at(N_X + x_at * N_Z + z_of(2)), :] = far_over_ref[turn]
        for at, (turn, distance) in enumerate(NEAR_BLOCKS):
            x_at = 1 - x if turn else x
            rows_ref[block_at(N_X + x_at * N_Z + z_of(-distance)), :] = near_over_ref[at]
        for step in range(steps):
            cols = pl.ds(step * STEP_ROWS, STEP_ROWS)
            scores = lax.dot_general(
                rows_ref[...], store_ref[cols, :], NT, preferred_element_type=jnp.float32
            )
            far_acc_ref[:, :, cols] = scores[: N_X * BLOCK].reshape(N_X, BLOCK, STEP_ROWS)
            over_acc_ref[:, :, :, cols] = scores[N_X * BLOCK :].reshape(N_X, N_Z, BLOCK, STEP_ROWS)
            for at, (source, target) in enumerate((
                (far_acc_ref.at[:, :, cols], out_ref.at[:, z_of(2), core, :, cols]),
                (over_acc_ref.at[:, :, :, cols], out_ref.at[:, :, 1 - core, :, cols]),
            )):
                copies.append(pltpu.make_async_copy(source, target, sems.at[step, at]))
                copies[-1].start()
        for copy in copies:
            copy.wait()

    vmem = pl.BlockSpec(memory_space=pltpu.VMEM)
    return pl.pallas_call(
        body,
        in_specs=[vmem] * 5,
        out_specs=pl.BlockSpec(memory_space=pl.ANY),
        out_shape=jax.ShapeDtypeStruct((N_X, N_Z, N_CORE, BLOCK, n_rows), jnp.float32),
        scratch_shapes=[
            pltpu.VMEM((N_X * (1 + N_Z) * BLOCK, width), jnp.bfloat16),
            pltpu.VMEM((N_X, BLOCK, n_rows), jnp.float32),
            pltpu.VMEM((N_X, N_Z, BLOCK, n_rows), jnp.float32),
            pltpu.SemaphoreType.DMA((N_NEAR,)),
            pltpu.SemaphoreType.DMA((steps, 2)),
        ],
        compiler_params=pltpu.CompilerParams(vmem_limit_bytes=10 << 20),
    )(near_scores, far, near_over, far_over, held)


def hold(stores):
    parts = 4
    size = stores.shape[0] // parts

    def body(store_ref, held_ref, sems):
        copies = []
        for part in range(parts):
            rows = pl.ds(part * size, size)
            copies.append(pltpu.make_async_copy(store_ref.at[rows], held_ref.at[rows], sems.at[part]))
            copies[-1].start()
        for copy in copies:
            copy.wait()

    return pl.pallas_call(
        body,
        in_specs=[pl.BlockSpec(memory_space=pl.ANY)],
        out_specs=pl.BlockSpec(memory_space=pltpu.VMEM),
        out_shape=jax.ShapeDtypeStruct(stores.shape, stores.dtype),
        scratch_shapes=[pltpu.SemaphoreType.DMA((parts,))],
        compiler_params=pltpu.CompilerParams(vmem_limit_bytes=4 << 20),
    )(pltpu.with_memory_space_constraint(stores, pltpu.HBM))


def partial_sums(activations, out_grads, query_ids, live, proj_in, proj_out):
    tok_rows, width = activations.shape
    n_left, n_right = proj_in.shape[1], proj_out.shape[1]
    parts = 2
    arrays = (query_ids.reshape(1, -1), proj_in.T, proj_out.T, out_grads, activations)
    size = tok_rows // parts

    def body(live_ref, *refs):
        small_refs, act_ref, sums_ref = refs[:4], refs[4], refs[5]
        held_refs = refs[6:10]
        rows_ref, left_ref, cells_ref, hot_ref, small_sems, sems = refs[10:]
        small_loads = []
        for at, (source, target) in enumerate(zip(small_refs, held_refs)):
            small_loads.append(pltpu.make_async_copy(source, target, small_sems.at[at]))
            small_loads[-1].start()
        ids_ref, in_ref, out_proj_ref, grad_ref = held_refs
        loads = []
        for part in range(parts):
            rows = pl.ds(part * size, size)
            loads.append(pltpu.make_async_copy(act_ref.at[rows], rows_ref.at[rows], sems.at[part]))
            loads[-1].start()
        small_loads[0].wait()
        swap = lax.rem(lax.axis_index("cell"), N_XH) * (Q // N_X)
        held_at = ids_ref[...] ^ swap
        hit = lax.broadcasted_iota(jnp.int32, (Q, tok_rows), 0) == held_at
        hot_ref[...] = jnp.where(hit, 1.0, 0.0).astype(jnp.bfloat16)
        for load in small_loads[1:]:
            load.wait()
        right = lax.dot_general(out_proj_ref[...], grad_ref[...], NT, preferred_element_type=jnp.float32)
        for part in range(parts):
            loads[part].wait()
            rows = pl.ds(part * size, size)
            left_ref[:, rows] = lax.dot_general(
                in_ref[...], rows_ref[rows, :], NT, preferred_element_type=jnp.float32
            )
        valid = lax.broadcasted_iota(jnp.int32, (1, tok_rows), 1) < live_ref[0]
        mask = jnp.where(valid, 1.0, 0.0)
        for at in range(n_left):
            cells = left_ref[at : at + 1, :] * right * mask
            cells_ref[at * n_right : (at + 1) * n_right, :] = cells.astype(jnp.bfloat16)
        sums = lax.dot_general(hot_ref[...], cells_ref[...], NT, preferred_element_type=jnp.float32)
        sums_ref[...] = sums.astype(jnp.bfloat16)

    vmem = pl.BlockSpec(memory_space=pltpu.VMEM)
    return pl.pallas_call(
        body,
        in_specs=[pl.BlockSpec(memory_space=pltpu.SMEM)] + [pl.BlockSpec(memory_space=pl.ANY)] * 5,
        out_specs=vmem,
        out_shape=jax.ShapeDtypeStruct((Q, n_left * n_right), jnp.bfloat16),
        scratch_shapes=[
            *(pltpu.VMEM(array.shape, array.dtype) for array in arrays[:4]),
            pltpu.VMEM((tok_rows, width), jnp.bfloat16),
            pltpu.VMEM((n_left, tok_rows), jnp.float32),
            pltpu.VMEM((n_left * n_right, tok_rows), jnp.bfloat16),
            pltpu.VMEM((Q, tok_rows), jnp.bfloat16),
            pltpu.SemaphoreType.DMA((4,)),
            pltpu.SemaphoreType.DMA((parts,)),
        ],
        compiler_params=pltpu.CompilerParams(vmem_limit_bytes=24 << 20),
    )(live, *(pltpu.with_memory_space_constraint(array, pltpu.HBM) for array in arrays))


def shards(activations, out_grads, query_ids, live, proj_in, proj_out, whitener, stores):
    partial_value = partial_sums(activations, out_grads, query_ids, live, proj_in, proj_out)
    pieces = lax.all_to_all(partial_value.reshape(N_TOK, BLOCK, -1), "tok", 0, 0, tiled=True)
    summed = pieces.astype(jnp.float32).sum(0).astype(jnp.bfloat16)
    total = jnp.dot(summed, whitener, preferred_element_type=jnp.float32)
    across = send(total.astype(jnp.bfloat16), SUM_X)
    held = hold(stores)
    total = total + across.astype(jnp.float32)
    rounded = total.astype(jnp.bfloat16)
    for piece in [send(rounded, route) for route in SUM_Y]:
        total = total + piece.astype(jnp.float32)
    return gather_and_score(total.astype(jnp.bfloat16), held)


def gather_and_score(own, held):
    here = (own, send(own, SWAP_X))
    up = tuple(send(piece, RING_A) for piece in here)
    down = tuple(send(piece, RING_B) for piece in here)
    far_own = send(up[0], RING_A)
    far_other = send(up[1], RING_A)
    near = jnp.stack([*here, *up, *down])
    near_over = send(near, SWAP_CORE)
    near_scores = score_near(near, held)
    far = jnp.stack([far_own, far_other])
    far_over = send(far, SWAP_CORE)
    return score_rest(near_scores, far, near_over, far_over, held).reshape(Q, -1)


def solution(mesh):
    in_specs = (
        P("tok", None),
        P("tok", None),
        P("tok"),
        P("tok"),
        P(None, "cell"),
        P(),
        P("cell", None),
        P(("tok", "cell"), None),
    )
    out_specs = P(None, ("tok", "cell"))
    return jax.shard_map(shards, mesh=mesh, in_specs=in_specs, out_specs=out_specs, check_vma=False)
```

time: 71.7 us -> 70 us (0.976)
  matrix products: 7.36 us -> 0.29 us
  Pallas kernels: 9.61 us -> 15.3 us
  starting transfers between devices: 21.1 us -> 20.2 us
  waiting for transfers between devices: 17.3 us -> 18.2 us
    dot_general x3 -> x0, matrix products: 7.08 us -> none  [the longest x1 5.67 us: shards(): jnp.dot(activations, proj_in, preferred_element_type=jnp.float32)]
    pallas_call x2 -> x3, Pallas kernels: 6.75 us -> 12.4 us  [the longest x1 6.61 us: partial_sums(): pl.pallas_call(body, in_specs=[pl.BlockSpec(memory_space=pltpu.SMEM)] + [...]
    ppermute x13, starting transfers between devices: 21.1 us -> 20.2 us  [send(): return lax.ppermute(value, AXES, route)]
    ppermute x13, waiting for transfers between devices: 17.3 us -> 18.2 us  [send(): return lax.ppermute(value, AXES, route)]
  transfers between devices with their start and end apart: 13 -> 13, of which waited for: 8 -> 8; matrix products, arithmetic and copies ran while one was open for 0% -> 0% of each run, Pallas kernels for 8% -> 7%
where the time goes in v2:
time: 70 us; the launch traced here: 69.8 us
  starting transfers between devices  20.2 us (29%)
  waiting for transfers between devices  18.2 us (26%)
  Pallas kernels  15.3 us (22%)
  blocking collectives  14.7 us (21%)
  between operations  0.86 us (1%)
    ppermute x13, starting transfers between devices, send(): return lax.ppermute(value, AXES, route)  20.2 us
    ppermute x13, waiting for transfers between devices, send(): return lax.ppermute(value, AXES, route)  18.2 us
    all_to_all x1, blocking collectives, shards(): lax.all_to_all(partial_value.reshape(N_TOK, BLOCK, -1), 'tok', 0, 0, tile...  14.7 us
    pallas_call x1, Pallas kernels, partial_sums(): pl.pallas_call(body, in_specs=[pl.BlockSpec(memory_space=pltpu.SMEM)] + [...  6.61 us
    pallas_call x1, Pallas kernels, score_rest(): pl.pallas_call(body, in_specs=[vmem] * 5, out_specs=pl.BlockSpec(memory_s...  3.6 us
    pallas_call x1, Pallas kernels, hold(): pl.pallas_call(body, in_specs=[pl.BlockSpec(memory_space=pl.ANY)], out_sp...  2.87 us
    pallas_call x1, Pallas kernels, score_near(): pl.pallas_call(body, in_specs=[vmem, vmem], out_specs=vmem, out_shape=jax...  2.22 us
  transfers between devices with their start and end apart: 13, of which 8 were waited for; matrix products, arithmetic and copies ran while one was open for 0% of the time, Pallas kernels for 7%

profile of v2, /device:TPU:1, one launch (start us, length us, event | category | flops | bytes accessed | tf_op | source)
XLA Modules:
  0.0 69.8 jit_solution(1219231305637184001)
XLA Ops:
  0.7 6.6 %shard_map.82 = bf16[512,256]{1,0:T(8,128)(2,1)S(1)} custom-call(s32[1]{0:T(128)S(6)} %copy.14.live_ref, s32[1,1024]{1,0:T(1,128)} %bitcast.26, bf16[8,4096]{1,0:T(8,128)(2,1)} %bitcast.24, bf16[32,1024]{1,0:T(8,128)(2,1)} %bitcast.25, bf16[1024,1024]{1,0:T(8,128)(2,1)} %refs_3_.1, bf16[1024,4096]{1,0:T(8,128)(2,1)} %refs_4_.1), custom_call_target="tpu_custom_call" | custom-call | tf_op jit(solution)/shard_map/pallas_call | solution.py:218
  7.4 14.7 %all_to_all.5 = bf16[16,32,256]{2,1,0:T(8,128)(2,1)S(1)} all-to-all(bf16[16,32,256]{2,1,0:T(8,128)(2,1)S(1)} %bitcast.21), channel_id=1, replica_groups=mesh['tok'=16,'cell'=8] {'tok'}, dimensions={0} | all-to-all | bytes 524288 | tf_op jit(solution)/shard_map/all_to_all | solution.py:238
  22.2 0.3 fusion.1
  22.4 2.1 %collective-permute-start = (bf16[32,2048]{1,0:T(8,128)(2,1)S(1)}, bf16[32,2048]{1,0:T(8,128)(2,1)S(1)}, u32[]{:S(2)}, u32[]{:S(2)}) collective-permute-start(bf16[32,2048]{1,0:T(8,128)(2,1)S(1)} %get-tuple-element.7), channel_id=1, source_target_pairs={{0,65},{1,64},{2,67},{3,66},{4,69},{5,68},{6,71},{7,70},{8,73},{9,... | collective-permute-start | bytes 393224 | tf_op jit(solution)/shard_map/ppermute | solution.py:46
  24.5 3.3 %collective-permute-done = bf16[32,2048]{1,0:T(8,128)(2,1)S(1)} collective-permute-done((bf16[32,2048]{1,0:T(8,128)(2,1)S(1)}, bf16[32,2048]{1,0:T(8,128)(2,1)S(1)}, u32[]{:S(2)}, u32[]{:S(2)}) %collective-permute-start) | collective-permute-done | bytes 131104 | tf_op jit(solution)/shard_map/ppermute | solution.py:46
  27.9 3.0 %collective-permute-start.3 = (bf16[32,2048]{1,0:T(8,128)(2,1)S(1)}, bf16[32,2048]{1,0:T(8,128)(2,1)S(1)}, u32[]{:S(2)}, u32[]{:S(2)}) collective-permute-start(bf16[32,2048]{1,0:T(8,128)(2,1)S(1)} %fusion), channel_id=1, source_target_pairs={{0,4},{1,5},{2,6},{3,7},{4,0},{5,1},{6,2},{7,3},{8,12},{9,13},{10,... | collective-permute-start | bytes 393224 | tf_op jit(solution)/shard_map/ppermute | solution.py:46
  30.9 0.4 collective-permute-start.2
  31.3 2.3 %collective-permute-start.1 = (bf16[32,2048]{1,0:T(8,128)(2,1)S(1)}, bf16[32,2048]{1,0:T(8,128)(2,1)S(1)}, u32[]{:S(2)}, u32[]{:S(2)}) collective-permute-start(bf16[32,2048]{1,0:T(8,128)(2,1)S(1)} %fusion), channel_id=1, source_target_pairs={{0,2},{1,3},{2,4},{3,5},{4,6},{5,7},{6,0},{7,1},{8,14},{9,15},{10,... | collective-permute-start | bytes 393224 | tf_op jit(solution)/shard_map/ppermute | solution.py:46
  33.6 3.6 %collective-permute-done.2 = bf16[32,2048]{1,0:T(8,128)(2,1)S(1)} collective-permute-done((bf16[32,2048]{1,0:T(8,128)(2,1)S(1)}, bf16[32,2048]{1,0:T(8,128)(2,1)S(1)}, u32[]{:S(2)}, u32[]{:S(2)}) %collective-permute-start.2) | collective-permute-done | bytes 131104 | tf_op jit(solution)/shard_map/ppermute | solution.py:46
  37.1 0.7 collective-permute-done.1
  37.9 0.1 collective-permute-start.4
  38.0 2.2 %collective-permute-start.5 = (bf16[32,2048]{1,0:T(8,128)(2,1)S(1)}, bf16[32,2048]{1,0:T(8,128)(2,1)S(1)}, u32[]{:S(2)}, u32[]{:S(2)}) collective-permute-start(bf16[32,2048]{1,0:T(8,128)(2,1)S(1)} %get-tuple-element.6), channel_id=1, source_target_pairs={{0,16},{1,17},{2,18},{3,19},{4,20},{5,21},{6,22},{7,23},{8,56},{9,... | collective-permute-start | bytes 393224 | tf_op jit(solution)/shard_map/ppermute | solution.py:46
  40.2 1.6 %collective-permute-done.4 = bf16[32,2048]{1,0:T(8,128)(2,1)S(1)} collective-permute-done((bf16[32,2048]{1,0:T(8,128)(2,1)S(1)}, bf16[32,2048]{1,0:T(8,128)(2,1)S(1)}, u32[]{:S(2)}, u32[]{:S(2)}) %collective-permute-start.4) | collective-permute-done | bytes 131104 | tf_op jit(solution)/shard_map/ppermute | solution.py:46
  41.8 0.9 %collective-permute-start.8 = (bf16[32,2048]{1,0:T(8,128)(2,1)S(1)}, bf16[32,2048]{1,0:T(8,128)(2,1)S(1)}, u32[]{:S(2)}, u32[]{:S(2)}) collective-permute-start(bf16[32,2048]{1,0:T(8,128)(2,1)S(1)} %collective-permute-done.4), channel_id=1, source_target_pairs={{0,48},{1,49},{2,50},{3,51},{4,52},{5,53},{6,54},{7,55},{8,24},{9,... | collective-permute-start | bytes 393224 | tf_op jit(solution)/shard_map/ppermute | solution.py:46
  42.7 1.8 %collective-permute-start.6 = (bf16[32,2048]{1,0:T(8,128)(2,1)S(1)}, bf16[32,2048]{1,0:T(8,128)(2,1)S(1)}, u32[]{:S(2)}, u32[]{:S(2)}) collective-permute-start(bf16[32,2048]{1,0:T(8,128)(2,1)S(1)} %collective-permute-done.4), channel_id=1, source_target_pairs={{0,16},{1,17},{2,18},{3,19},{4,20},{5,21},{6,22},{7,23},{8,56},{9,... | collective-permute-start | bytes 393224 | tf_op jit(solution)/shard_map/ppermute | solution.py:46
  44.5 2.6 %collective-permute-done.6 = bf16[32,2048]{1,0:T(8,128)(2,1)S(1)} collective-permute-done((bf16[32,2048]{1,0:T(8,128)(2,1)S(1)}, bf16[32,2048]{1,0:T(8,128)(2,1)S(1)}, u32[]{:S(2)}, u32[]{:S(2)}) %collective-permute-start.6) | collective-permute-done | bytes 131104 | tf_op jit(solution)/shard_map/ppermute | solution.py:46
  47.2 0.8 %collective-permute-done.8 = bf16[32,2048]{1,0:T(8,128)(2,1)S(1)} collective-permute-done((bf16[32,2048]{1,0:T(8,128)(2,1)S(1)}, bf16[32,2048]{1,0:T(8,128)(2,1)S(1)}, u32[]{:S(2)}, u32[]{:S(2)}) %collective-permute-start.8) | collective-permute-done | bytes 131104 | tf_op jit(solution)/shard_map/ppermute | solution.py:46
  48.0 5.3 %collective-permute-start.11 = (bf16[6,32,2048]{2,1,0:T(8,128)(2,1)S(1)}, bf16[6,32,2048]{2,1,0:T(8,128)(2,1)S(1)}, u32[]{:S(2)}, u32[]{:S(2)}) collective-permute-start(bf16[6,32,2048]{2,1,0:T(8,128)(2,1)S(1)} %bitcast_dynamic-update-slice_fusion.near_ref), channel_id=1, source_target_pairs={{0,8},{1,9},{2,10},{3,11},{4,12},{5,13},{6,14},{7,15},{8,0},{9,1},... | collective-permute-start | bytes 2359304 | tf_op jit(solution)/shard_map/ppermute | solution.py:46
  53.3 3.8 %collective-permute-done.9 = bf16[32,2048]{1,0:T(8,128)(2,1)S(1)} collective-permute-done((bf16[32,2048]{1,0:T(8,128)(2,1)S(1)}, bf16[32,2048]{1,0:T(8,128)(2,1)S(1)}, u32[]{:S(2)}, u32[]{:S(2)}) %collective-permute-start.9) | collective-permute-done | bytes 131104 | tf_op jit(solution)/shard_map/ppermute | solution.py:46
  57.1 1.7 %collective-permute-done.10 = bf16[32,2048]{1,0:T(8,128)(2,1)S(1)} collective-permute-done((bf16[32,2048]{1,0:T(8,128)(2,1)S(1)}, bf16[32,2048]{1,0:T(8,128)(2,1)S(1)}, u32[]{:S(2)}, u32[]{:S(2)}) %collective-permute-start.10) | collective-permute-done | bytes 131104 | tf_op jit(solution)/shard_map/ppermute | solution.py:46
  58.9 2.2 %collective-permute-start.12 = (bf16[2,32,2048]{2,1,0:T(8,128)(2,1)S(1)}, bf16[2,32,2048]{2,1,0:T(8,128)(2,1)S(1)}, u32[]{:S(2)}, u32[]{:S(2)}) collective-permute-start(bf16[2,32,2048]{2,1,0:T(8,128)(2,1)S(1)} %pad_maximum_fusion.far_ref), channel_id=1, source_target_pairs={{0,8},{1,9},{2,10},{3,11},{4,12},{5,13},{6,14},{7,15},{8,0},{9,1},... | collective-permute-start | bytes 786440 | tf_op jit(solution)/shard_map/ppermute | solution.py:46
  61.1 2.9 %shard_map.83.store_ref = bf16[1536,2048]{1,0:T(8,128)(2,1)S(1)} custom-call(bf16[1536,2048]{1,0:T(8,128)(2,1)} %store_ref.1), custom_call_target="tpu_custom_call" | custom-call | tf_op jit(solution)/shard_map/pallas_call | solution.py:164
  64.0 2.2 %shard_map.84.near_scores_ref = f32[3,2,32,1536]{3,2,1,0:T(8,128)S(1)} custom-call(bf16[6,32,2048]{2,1,0:T(8,128)(2,1)S(1)} %bitcast_dynamic-update-slice_fusion.near_ref, bf16[1536,2048]{1,0:T(8,128)(2,1)S(1)} %shard_map.83.store_ref), custom_call_target="tpu_custom_call" | custom-call | tf_op jit(solution)/shard_map/pallas_call | solution.py:85
  66.2 3.6 %shard_map.85 = f32[2,4,2,32,1536]{4,3,2,1,0:T(8,128)} custom-call(f32[3,2,32,1536]{3,2,1,0:T(8,128)S(1)} %shard_map.84.near_scores_ref, bf16[2,32,2048]{2,1,0:T(8,128)(2,1)S(1)} %pad_maximum_fusion.far_ref, bf16[6,32,2048]{2,1,0:T(8,128)(2,1)S(1)} %collective-permute-done.11.near_over_ref, bf16[2,32,2048]{2,1,0:T(8,128)(2,1)S(1)} %collective-permute-done.12.far_over_ref, ...), custom_call_target="tpu_custom_call" | custom-call | tf_op jit(solution)/shard_map/pallas_call | solution.py:135
  (19 shorter events, 0.2 us)
Async XLA Ops:
  0.0 22.1 %copy-start = (bf16[256,2048]{1,0:T(8,128)(2,1)S(1)}, bf16[256,2048]{1,0:T(8,128)(2,1)}, u32[]{:S(2)}) copy-start(bf16[256,2048]{1,0:T(8,128)(2,1)} %param.14) | copy-start | bytes 3145732
  22.4 5.4 %collective-permute-start = (bf16[32,2048]{1,0:T(8,128)(2,1)S(1)}, bf16[32,2048]{1,0:T(8,128)(2,1)S(1)}, u32[]{:S(2)}, u32[]{:S(2)}) collective-permute-start(bf16[32,2048]{1,0:T(8,128)(2,1)S(1)} %get-tuple-element.7), channel_id=1, source_target_pairs={{0,65},{1,64},{2,67},{3,66},{4,69},{5,68},{6,71},{7,70},{8,73},{9,... | collective-permute-start | bytes 393224 | tf_op jit(solution)/shard_map/ppermute | solution.py:46
  27.9 5.7 %collective-permute-start.3 = (bf16[32,2048]{1,0:T(8,128)(2,1)S(1)}, bf16[32,2048]{1,0:T(8,128)(2,1)S(1)}, u32[]{:S(2)}, u32[]{:S(2)}) collective-permute-start(bf16[32,2048]{1,0:T(8,128)(2,1)S(1)} %fusion), channel_id=1, source_target_pairs={{0,4},{1,5},{2,6},{3,7},{4,0},{5,1},{6,2},{7,3},{8,12},{9,13},{10,... | collective-permute-start | bytes 393224 | tf_op jit(solution)/shard_map/ppermute | solution.py:46
  30.9 6.2 %collective-permute-start.2 = (bf16[32,2048]{1,0:T(8,128)(2,1)S(1)}, bf16[32,2048]{1,0:T(8,128)(2,1)S(1)}, u32[]{:S(2)}, u32[]{:S(2)}) collective-permute-start(bf16[32,2048]{1,0:T(8,128)(2,1)S(1)} %fusion), channel_id=1, source_target_pairs={{0,6},{1,7},{2,0},{3,1},{4,2},{5,3},{6,4},{7,5},{8,10},{9,11},{10,... | collective-permute-start | bytes 393224 | tf_op jit(solution)/shard_map/ppermute | solution.py:46
  31.3 6.5 %collective-permute-start.1 = (bf16[32,2048]{1,0:T(8,128)(2,1)S(1)}, bf16[32,2048]{1,0:T(8,128)(2,1)S(1)}, u32[]{:S(2)}, u32[]{:S(2)}) collective-permute-start(bf16[32,2048]{1,0:T(8,128)(2,1)S(1)} %fusion), channel_id=1, source_target_pairs={{0,2},{1,3},{2,4},{3,5},{4,6},{5,7},{6,0},{7,1},{8,14},{9,15},{10,... | collective-permute-start | bytes 393224 | tf_op jit(solution)/shard_map/ppermute | solution.py:46
  37.9 3.9 %collective-permute-start.4 = (bf16[32,2048]{1,0:T(8,128)(2,1)S(1)}, bf16[32,2048]{1,0:T(8,128)(2,1)S(1)}, u32[]{:S(2)}, u32[]{:S(2)}) collective-permute-start(bf16[32,2048]{1,0:T(8,128)(2,1)S(1)} %get-tuple-element.6), channel_id=1, source_target_pairs={{0,64},{1,65},{2,66},{3,67},{4,68},{5,69},{6,70},{7,71},{8,72},{9,... | collective-permute-start | bytes 393224 | tf_op jit(solution)/shard_map/ppermute | solution.py:46
  38.0 6.5 %collective-permute-start.5 = (bf16[32,2048]{1,0:T(8,128)(2,1)S(1)}, bf16[32,2048]{1,0:T(8,128)(2,1)S(1)}, u32[]{:S(2)}, u32[]{:S(2)}) collective-permute-start(bf16[32,2048]{1,0:T(8,128)(2,1)S(1)} %get-tuple-element.6), channel_id=1, source_target_pairs={{0,16},{1,17},{2,18},{3,19},{4,20},{5,21},{6,22},{7,23},{8,56},{9,... | collective-permute-start | bytes 393224 | tf_op jit(solution)/shard_map/ppermute | solution.py:46
  40.1 7.0 %collective-permute-start.7 = (bf16[32,2048]{1,0:T(8,128)(2,1)S(1)}, bf16[32,2048]{1,0:T(8,128)(2,1)S(1)}, u32[]{:S(2)}, u32[]{:S(2)}) collective-permute-start(bf16[32,2048]{1,0:T(8,128)(2,1)S(1)} %get-tuple-element.6), channel_id=1, source_target_pairs={{0,48},{1,49},{2,50},{3,51},{4,52},{5,53},{6,54},{7,55},{8,24},{9,... | collective-permute-start | bytes 393224 | tf_op jit(solution)/shard_map/ppermute | solution.py:46
  41.8 6.2 %collective-permute-start.8 = (bf16[32,2048]{1,0:T(8,128)(2,1)S(1)}, bf16[32,2048]{1,0:T(8,128)(2,1)S(1)}, u32[]{:S(2)}, u32[]{:S(2)}) collective-permute-start(bf16[32,2048]{1,0:T(8,128)(2,1)S(1)} %collective-permute-done.4), channel_id=1, source_target_pairs={{0,48},{1,49},{2,50},{3,51},{4,52},{5,53},{6,54},{7,55},{8,24},{9,... | collective-permute-start | bytes 393224 | tf_op jit(solution)/shard_map/ppermute | solution.py:46
  42.7 4.5 %collective-permute-start.6 = (bf16[32,2048]{1,0:T(8,128)(2,1)S(1)}, bf16[32,2048]{1,0:T(8,128)(2,1)S(1)}, u32[]{:S(2)}, u32[]{:S(2)}) collective-permute-start(bf16[32,2048]{1,0:T(8,128)(2,1)S(1)} %collective-permute-done.4), channel_id=1, source_target_pairs={{0,16},{1,17},{2,18},{3,19},{4,20},{5,21},{6,22},{7,23},{8,56},{9,... | collective-permute-start | bytes 393224 | tf_op jit(solution)/shard_map/ppermute | solution.py:46
  48.0 18.2 %collective-permute-start.11 = (bf16[6,32,2048]{2,1,0:T(8,128)(2,1)S(1)}, bf16[6,32,2048]{2,1,0:T(8,128)(2,1)S(1)}, u32[]{:S(2)}, u32[]{:S(2)}) collective-permute-start(bf16[6,32,2048]{2,1,0:T(8,128)(2,1)S(1)} %bitcast_dynamic-update-slice_fusion.near_ref), channel_id=1, source_target_pairs={{0,8},{1,9},{2,10},{3,11},{4,12},{5,13},{6,14},{7,15},{8,0},{9,1},... | collective-permute-start | bytes 2359304 | tf_op jit(solution)/shard_map/ppermute | solution.py:46
  53.3 3.8 %collective-permute-start.9 = (bf16[32,2048]{1,0:T(8,128)(2,1)S(1)}, bf16[32,2048]{1,0:T(8,128)(2,1)S(1)}, u32[]{:S(2)}, u32[]{:S(2)}) collective-permute-start(bf16[32,2048]{1,0:T(8,128)(2,1)S(1)} %collective-permute-done.5), channel_id=1, source_target_pairs={{0,16},{1,17},{2,18},{3,19},{4,20},{5,21},{6,22},{7,23},{8,56},{9,... | collective-permute-start | bytes 393224 | tf_op jit(solution)/shard_map/ppermute | solution.py:46
  53.3 5.5 %collective-permute-start.10 = (bf16[32,2048]{1,0:T(8,128)(2,1)S(1)}, bf16[32,2048]{1,0:T(8,128)(2,1)S(1)}, u32[]{:S(2)}, u32[]{:S(2)}) collective-permute-start(bf16[32,2048]{1,0:T(8,128)(2,1)S(1)} %collective-permute-done.6), channel_id=1, source_target_pairs={{0,16},{1,17},{2,18},{3,19},{4,20},{5,21},{6,22},{7,23},{8,56},{9,... | collective-permute-start | bytes 393224 | tf_op jit(solution)/shard_map/ppermute | solution.py:46
  58.9 7.3 %collective-permute-start.12 = (bf16[2,32,2048]{2,1,0:T(8,128)(2,1)S(1)}, bf16[2,32,2048]{2,1,0:T(8,128)(2,1)S(1)}, u32[]{:S(2)}, u32[]{:S(2)}) collective-permute-start(bf16[2,32,2048]{2,1,0:T(8,128)(2,1)S(1)} %pad_maximum_fusion.far_ref), channel_id=1, source_target_pairs={{0,8},{1,9},{2,10},{3,11},{4,12},{5,13},{6,14},{7,15},{8,0},{9,1},... | collective-permute-start | bytes 786440 | tf_op jit(solution)/shard_map/ppermute | solution.py:46

commit v3 on v2

--- a/solution.py
+++ b/solution.py
@@ -97,7 +97,7 @@
     steps = n_rows // STEP_ROWS
 
     def body(
-        near_scores_ref, far_ref, near_over_ref, far_over_ref, store_ref, out_ref,
+        near_scores_ref, far_0, far_1, near_over_ref, far_over_0, far_over_1, store_ref, out_ref,
         rows_ref, far_acc_ref, over_acc_ref, near_sems, sems,
     ):
         x, z_of, core = place()
@@ -110,8 +110,8 @@
             copies[-1].start()
         for turn in range(N_X):
             x_at = 1 - x if turn else x
-            rows_ref[block_at(x_at), :] = far_ref[turn]
-            rows_ref[block_at(N_X + x_at * N_Z + z_of(2)), :] = far_over_ref[turn]
+            rows_ref[block_at(x_at), :] = (far_0, far_1)[turn][...]
+            rows_ref[block_at(N_X + x_at * N_Z + z_of(2)), :] = (far_over_0, far_over_1)[turn][...]
         for at, (turn, distance) in enumerate(NEAR_BLOCKS):
             x_at = 1 - x if turn else x
             rows_ref[block_at(N_X + x_at * N_Z + z_of(-distance)), :] = near_over_ref[at]
@@ -134,7 +134,7 @@
     vmem = pl.BlockSpec(memory_space=pltpu.VMEM)
     return pl.pallas_call(
         body,
-        in_specs=[vmem] * 5,
+        in_specs=[vmem] * 7,
         out_specs=pl.BlockSpec(memory_space=pl.ANY),
         out_shape=jax.ShapeDtypeStruct((N_X, N_Z, N_CORE, BLOCK, n_rows), jnp.float32),
         scratch_shapes=[
@@ -145,7 +145,7 @@
             pltpu.SemaphoreType.DMA((steps, 2)),
         ],
         compiler_params=pltpu.CompilerParams(vmem_limit_bytes=10 << 20),
-    )(near_scores, far, near_over, far_over, held)
+    )(near_scores, *far, near_over, *far_over, held)
 
 
 def hold(stores):
@@ -256,8 +256,8 @@
     near = jnp.stack([*here, *up, *down])
     near_over = send(near, SWAP_CORE)
     near_scores = score_near(near, held)
-    far = jnp.stack([far_own, far_other])
-    far_over = send(far, SWAP_CORE)
+    far = (far_own, far_other)
+    far_over = tuple(send(piece, SWAP_CORE) for piece in far)
     return score_rest(near_scores, far, near_over, far_over, held).reshape(Q, -1)
 
 

time: 70 us -> 69.9 us (level)
  starting transfers between devices: 20.2 us -> 21.9 us
  waiting for transfers between devices: 18.2 us -> 16.5 us
    ppermute x13 -> x14, waiting for transfers between devices: 18.2 us -> 16.5 us  [send(): return lax.ppermute(value, AXES, route)]
    ppermute x13 -> x14, starting transfers between devices: 20.2 us -> 21.9 us  [send(): return lax.ppermute(value, AXES, route)]
  transfers between devices with their start and end apart: 13 -> 14, of which waited for: 8 -> 7; matrix products, arithmetic and copies ran while one was open for 0% -> 0% of each run, Pallas kernels for 7% -> 7%
where the time goes in v3:
time: 69.9 us; the launch traced here: 69.7 us
  starting transfers between devices  21.9 us (31%)
  waiting for transfers between devices  16.5 us (24%)
  Pallas kernels  15.3 us (22%)
  blocking collectives  14.7 us (21%)
  between operations  0.87 us (1%)
    ppermute x14, starting transfers between devices, send(): return lax.ppermute(value, AXES, route)  21.9 us
    ppermute x14, waiting for transfers between devices, send(): return lax.ppermute(value, AXES, route)  16.5 us
    all_to_all x1, blocking collectives, shards(): lax.all_to_all(partial_value.reshape(N_TOK, BLOCK, -1), 'tok', 0, 0, tile...  14.7 us
    pallas_call x1, Pallas kernels, partial_sums(): pl.pallas_call(body, in_specs=[pl.BlockSpec(memory_space=pltpu.SMEM)] + [...  6.61 us
    pallas_call x1, Pallas kernels, score_rest(): pl.pallas_call(body, in_specs=[vmem] * 7, out_specs=pl.BlockSpec(memory_s...  3.6 us
    pallas_call x1, Pallas kernels, hold(): pl.pallas_call(body, in_specs=[pl.BlockSpec(memory_space=pl.ANY)], out_sp...  2.87 us
    pallas_call x1, Pallas kernels, score_near(): pl.pallas_call(body, in_specs=[vmem, vmem], out_specs=vmem, out_shape=jax...  2.21 us
  transfers between devices with their start and end apart: 14, of which 7 were waited for; matrix products, arithmetic and copies ran while one was open for 0% of the time, Pallas kernels for 7%

profile of v3, /device:TPU:1, one launch (start us, length us, event | category | flops | bytes accessed | tf_op | source)
XLA Modules:
  0.0 69.7 jit_solution(8287454684199621020)
XLA Ops:
  0.7 6.6 %shard_map.82 = bf16[512,256]{1,0:T(8,128)(2,1)S(1)} custom-call(s32[1]{0:T(128)S(6)} %copy.14.live_ref, s32[1,1024]{1,0:T(1,128)} %bitcast.22, bf16[8,4096]{1,0:T(8,128)(2,1)} %bitcast.20, bf16[32,1024]{1,0:T(8,128)(2,1)} %bitcast.21, bf16[1024,1024]{1,0:T(8,128)(2,1)} %refs_3_.1, bf16[1024,4096]{1,0:T(8,128)(2,1)} %refs_4_.1), custom_call_target="tpu_custom_call" | custom-call | tf_op jit(solution)/shard_map/pallas_call | solution.py:218
  7.4 14.7 %all_to_all.5 = bf16[16,32,256]{2,1,0:T(8,128)(2,1)S(1)} all-to-all(bf16[16,32,256]{2,1,0:T(8,128)(2,1)S(1)} %bitcast.19), channel_id=1, replica_groups=mesh['tok'=16,'cell'=8] {'tok'}, dimensions={0} | all-to-all | bytes 524288 | tf_op jit(solution)/shard_map/all_to_all | solution.py:238
  22.2 0.3 fusion.1
  22.4 2.1 %collective-permute-start = (bf16[32,2048]{1,0:T(8,128)(2,1)S(1)}, bf16[32,2048]{1,0:T(8,128)(2,1)S(1)}, u32[]{:S(2)}, u32[]{:S(2)}) collective-permute-start(bf16[32,2048]{1,0:T(8,128)(2,1)S(1)} %get-tuple-element.7), channel_id=1, source_target_pairs={{0,65},{1,64},{2,67},{3,66},{4,69},{5,68},{6,71},{7,70},{8,73},{9,... | collective-permute-start | bytes 393224 | tf_op jit(solution)/shard_map/ppermute | solution.py:46
  24.5 3.3 %collective-permute-done = bf16[32,2048]{1,0:T(8,128)(2,1)S(1)} collective-permute-done((bf16[32,2048]{1,0:T(8,128)(2,1)S(1)}, bf16[32,2048]{1,0:T(8,128)(2,1)S(1)}, u32[]{:S(2)}, u32[]{:S(2)}) %collective-permute-start) | collective-permute-done | bytes 131104 | tf_op jit(solution)/shard_map/ppermute | solution.py:46
  27.9 3.0 %collective-permute-start.3 = (bf16[32,2048]{1,0:T(8,128)(2,1)S(1)}, bf16[32,2048]{1,0:T(8,128)(2,1)S(1)}, u32[]{:S(2)}, u32[]{:S(2)}) collective-permute-start(bf16[32,2048]{1,0:T(8,128)(2,1)S(1)} %fusion), channel_id=1, source_target_pairs={{0,4},{1,5},{2,6},{3,7},{4,0},{5,1},{6,2},{7,3},{8,12},{9,13},{10,... | collective-permute-start | bytes 393224 | tf_op jit(solution)/shard_map/ppermute | solution.py:46
  30.9 0.4 collective-permute-start.2
  31.3 2.3 %collective-permute-start.1 = (bf16[32,2048]{1,0:T(8,128)(2,1)S(1)}, bf16[32,2048]{1,0:T(8,128)(2,1)S(1)}, u32[]{:S(2)}, u32[]{:S(2)}) collective-permute-start(bf16[32,2048]{1,0:T(8,128)(2,1)S(1)} %fusion), channel_id=1, source_target_pairs={{0,2},{1,3},{2,4},{3,5},{4,6},{5,7},{6,0},{7,1},{8,14},{9,15},{10,... | collective-permute-start | bytes 393224 | tf_op jit(solution)/shard_map/ppermute | solution.py:46
  33.6 3.6 %collective-permute-done.2 = bf16[32,2048]{1,0:T(8,128)(2,1)S(1)} collective-permute-done((bf16[32,2048]{1,0:T(8,128)(2,1)S(1)}, bf16[32,2048]{1,0:T(8,128)(2,1)S(1)}, u32[]{:S(2)}, u32[]{:S(2)}) %collective-permute-start.2) | collective-permute-done | bytes 131104 | tf_op jit(solution)/shard_map/ppermute | solution.py:46
  37.1 0.7 collective-permute-done.1
  37.9 0.1 collective-permute-start.4
  38.0 2.2 %collective-permute-start.5 = (bf16[32,2048]{1,0:T(8,128)(2,1)S(1)}, bf16[32,2048]{1,0:T(8,128)(2,1)S(1)}, u32[]{:S(2)}, u32[]{:S(2)}) collective-permute-start(bf16[32,2048]{1,0:T(8,128)(2,1)S(1)} %get-tuple-element.6), channel_id=1, source_target_pairs={{0,16},{1,17},{2,18},{3,19},{4,20},{5,21},{6,22},{7,23},{8,56},{9,... | collective-permute-start | bytes 393224 | tf_op jit(solution)/shard_map/ppermute | solution.py:46
  40.2 1.6 %collective-permute-done.4 = bf16[32,2048]{1,0:T(8,128)(2,1)S(1)} collective-permute-done((bf16[32,2048]{1,0:T(8,128)(2,1)S(1)}, bf16[32,2048]{1,0:T(8,128)(2,1)S(1)}, u32[]{:S(2)}, u32[]{:S(2)}) %collective-permute-start.4) | collective-permute-done | bytes 131104 | tf_op jit(solution)/shard_map/ppermute | solution.py:46
  41.8 0.9 %collective-permute-start.8 = (bf16[32,2048]{1,0:T(8,128)(2,1)S(1)}, bf16[32,2048]{1,0:T(8,128)(2,1)S(1)}, u32[]{:S(2)}, u32[]{:S(2)}) collective-permute-start(bf16[32,2048]{1,0:T(8,128)(2,1)S(1)} %collective-permute-done.4), channel_id=1, source_target_pairs={{0,48},{1,49},{2,50},{3,51},{4,52},{5,53},{6,54},{7,55},{8,24},{9,... | collective-permute-start | bytes 393224 | tf_op jit(solution)/shard_map/ppermute | solution.py:46
  42.7 1.8 %collective-permute-start.6 = (bf16[32,2048]{1,0:T(8,128)(2,1)S(1)}, bf16[32,2048]{1,0:T(8,128)(2,1)S(1)}, u32[]{:S(2)}, u32[]{:S(2)}) collective-permute-start(bf16[32,2048]{1,0:T(8,128)(2,1)S(1)} %collective-permute-done.4), channel_id=1, source_target_pairs={{0,16},{1,17},{2,18},{3,19},{4,20},{5,21},{6,22},{7,23},{8,56},{9,... | collective-permute-start | bytes 393224 | tf_op jit(solution)/shard_map/ppermute | solution.py:46
  44.5 2.6 %collective-permute-done.6 = bf16[32,2048]{1,0:T(8,128)(2,1)S(1)} collective-permute-done((bf16[32,2048]{1,0:T(8,128)(2,1)S(1)}, bf16[32,2048]{1,0:T(8,128)(2,1)S(1)}, u32[]{:S(2)}, u32[]{:S(2)}) %collective-permute-start.6) | collective-permute-done | bytes 131104 | tf_op jit(solution)/shard_map/ppermute | solution.py:46
  47.2 0.8 %collective-permute-done.8 = bf16[32,2048]{1,0:T(8,128)(2,1)S(1)} collective-permute-done((bf16[32,2048]{1,0:T(8,128)(2,1)S(1)}, bf16[32,2048]{1,0:T(8,128)(2,1)S(1)}, u32[]{:S(2)}, u32[]{:S(2)}) %collective-permute-start.8) | collective-permute-done | bytes 131104 | tf_op jit(solution)/shard_map/ppermute | solution.py:46
  48.0 5.3 %collective-permute-start.11 = (bf16[6,32,2048]{2,1,0:T(8,128)(2,1)S(1)}, bf16[6,32,2048]{2,1,0:T(8,128)(2,1)S(1)}, u32[]{:S(2)}, u32[]{:S(2)}) collective-permute-start(bf16[6,32,2048]{2,1,0:T(8,128)(2,1)S(1)} %bitcast_dynamic-update-slice_fusion.near_ref), channel_id=1, source_target_pairs={{0,8},{1,9},{2,10},{3,11},{4,12},{5,13},{6,14},{7,15},{8,0},{9,1},... | collective-permute-start | bytes 2359304 | tf_op jit(solution)/shard_map/ppermute | solution.py:46
  53.3 3.8 %collective-permute-done.9.far_0 = bf16[32,2048]{1,0:T(8,128)(2,1)S(1)} collective-permute-done((bf16[32,2048]{1,0:T(8,128)(2,1)S(1)}, bf16[32,2048]{1,0:T(8,128)(2,1)S(1)}, u32[]{:S(2)}, u32[]{:S(2)}) %collective-permute-start.9) | collective-permute-done | bytes 131104 | tf_op jit(solution)/shard_map/ppermute | solution.py:46
  57.1 2.4 %collective-permute-start.12 = (bf16[32,2048]{1,0:T(8,128)(2,1)S(1)}, bf16[32,2048]{1,0:T(8,128)(2,1)S(1)}, u32[]{:S(2)}, u32[]{:S(2)}) collective-permute-start(bf16[32,2048]{1,0:T(8,128)(2,1)S(1)} %collective-permute-done.9.far_0), channel_id=1, source_target_pairs={{0,8},{1,9},{2,10},{3,11},{4,12},{5,13},{6,14},{7,15},{8,0},{9,1},... | collective-permute-start | bytes 393224 | tf_op jit(solution)/shard_map/ppermute | solution.py:46
  59.6 1.4 %collective-permute-start.13 = (bf16[32,2048]{1,0:T(8,128)(2,1)S(1)}, bf16[32,2048]{1,0:T(8,128)(2,1)S(1)}, u32[]{:S(2)}, u32[]{:S(2)}) collective-permute-start(bf16[32,2048]{1,0:T(8,128)(2,1)S(1)} %collective-permute-done.10.far_1), channel_id=1, source_target_pairs={{0,8},{1,9},{2,10},{3,11},{4,12},{5,13},{6,14},{7,15},{8,0},{9,1},... | collective-permute-start | bytes 393224 | tf_op jit(solution)/shard_map/ppermute | solution.py:46
  61.0 2.9 %shard_map.83.store_ref = bf16[1536,2048]{1,0:T(8,128)(2,1)S(1)} custom-call(bf16[1536,2048]{1,0:T(8,128)(2,1)} %store_ref.1), custom_call_target="tpu_custom_call" | custom-call | tf_op jit(solution)/shard_map/pallas_call | solution.py:164
  63.9 2.2 %shard_map.84.near_scores_ref = f32[3,2,32,1536]{3,2,1,0:T(8,128)S(1)} custom-call(bf16[6,32,2048]{2,1,0:T(8,128)(2,1)S(1)} %bitcast_dynamic-update-slice_fusion.near_ref, bf16[1536,2048]{1,0:T(8,128)(2,1)S(1)} %shard_map.83.store_ref), custom_call_target="tpu_custom_call" | custom-call | tf_op jit(solution)/shard_map/pallas_call | solution.py:85
  66.1 3.6 %shard_map.85 = f32[2,4,2,32,1536]{4,3,2,1,0:T(8,128)} custom-call(f32[3,2,32,1536]{3,2,1,0:T(8,128)S(1)} %shard_map.84.near_scores_ref, bf16[32,2048]{1,0:T(8,128)(2,1)S(1)} %collective-permute-done.9.far_0, bf16[32,2048]{1,0:T(8,128)(2,1)S(1)} %collective-permute-done.10.far_1, bf16[6,32,2048]{2,1,0:T(8,128)(2,1)S(1)} %collective-permute-done.11.near_over_ref, ...), custom_call_target="tpu_custom_call" | custom-call | tf_op jit(solution)/shard_map/pallas_call | solution.py:135
  (20 shorter events, 0.2 us)
Async XLA Ops:
  0.0 22.1 %copy-start = (bf16[256,2048]{1,0:T(8,128)(2,1)S(1)}, bf16[256,2048]{1,0:T(8,128)(2,1)}, u32[]{:S(2)}) copy-start(bf16[256,2048]{1,0:T(8,128)(2,1)} %param.14) | copy-start | bytes 3145732
  22.4 5.4 %collective-permute-start = (bf16[32,2048]{1,0:T(8,128)(2,1)S(1)}, bf16[32,2048]{1,0:T(8,128)(2,1)S(1)}, u32[]{:S(2)}, u32[]{:S(2)}) collective-permute-start(bf16[32,2048]{1,0:T(8,128)(2,1)S(1)} %get-tuple-element.7), channel_id=1, source_target_pairs={{0,65},{1,64},{2,67},{3,66},{4,69},{5,68},{6,71},{7,70},{8,73},{9,... | collective-permute-start | bytes 393224 | tf_op jit(solution)/shard_map/ppermute | solution.py:46
  27.9 5.7 %collective-permute-start.3 = (bf16[32,2048]{1,0:T(8,128)(2,1)S(1)}, bf16[32,2048]{1,0:T(8,128)(2,1)S(1)}, u32[]{:S(2)}, u32[]{:S(2)}) collective-permute-start(bf16[32,2048]{1,0:T(8,128)(2,1)S(1)} %fusion), channel_id=1, source_target_pairs={{0,4},{1,5},{2,6},{3,7},{4,0},{5,1},{6,2},{7,3},{8,12},{9,13},{10,... | collective-permute-start | bytes 393224 | tf_op jit(solution)/shard_map/ppermute | solution.py:46
  30.9 6.2 %collective-permute-start.2 = (bf16[32,2048]{1,0:T(8,128)(2,1)S(1)}, bf16[32,2048]{1,0:T(8,128)(2,1)S(1)}, u32[]{:S(2)}, u32[]{:S(2)}) collective-permute-start(bf16[32,2048]{1,0:T(8,128)(2,1)S(1)} %fusion), channel_id=1, source_target_pairs={{0,6},{1,7},{2,0},{3,1},{4,2},{5,3},{6,4},{7,5},{8,10},{9,11},{10,... | collective-permute-start | bytes 393224 | tf_op jit(solution)/shard_map/ppermute | solution.py:46
  31.3 6.5 %collective-permute-start.1 = (bf16[32,2048]{1,0:T(8,128)(2,1)S(1)}, bf16[32,2048]{1,0:T(8,128)(2,1)S(1)}, u32[]{:S(2)}, u32[]{:S(2)}) collective-permute-start(bf16[32,2048]{1,0:T(8,128)(2,1)S(1)} %fusion), channel_id=1, source_target_pairs={{0,2},{1,3},{2,4},{3,5},{4,6},{5,7},{6,0},{7,1},{8,14},{9,15},{10,... | collective-permute-start | bytes 393224 | tf_op jit(solution)/shard_map/ppermute | solution.py:46
  37.9 3.9 %collective-permute-start.4 = (bf16[32,2048]{1,0:T(8,128)(2,1)S(1)}, bf16[32,2048]{1,0:T(8,128)(2,1)S(1)}, u32[]{:S(2)}, u32[]{:S(2)}) collective-permute-start(bf16[32,2048]{1,0:T(8,128)(2,1)S(1)} %get-tuple-element.6), channel_id=1, source_target_pairs={{0,64},{1,65},{2,66},{3,67},{4,68},{5,69},{6,70},{7,71},{8,72},{9,... | collective-permute-start | bytes 393224 | tf_op jit(solution)/shard_map/ppermute | solution.py:46
  38.0 6.5 %collective-permute-start.5 = (bf16[32,2048]{1,0:T(8,128)(2,1)S(1)}, bf16[32,2048]{1,0:T(8,128)(2,1)S(1)}, u32[]{:S(2)}, u32[]{:S(2)}) collective-permute-start(bf16[32,2048]{1,0:T(8,128)(2,1)S(1)} %get-tuple-element.6), channel_id=1, source_target_pairs={{0,16},{1,17},{2,18},{3,19},{4,20},{5,21},{6,22},{7,23},{8,56},{9,... | collective-permute-start | bytes 393224 | tf_op jit(solution)/shard_map/ppermute | solution.py:46
  40.1 7.0 %collective-permute-start.7 = (bf16[32,2048]{1,0:T(8,128)(2,1)S(1)}, bf16[32,2048]{1,0:T(8,128)(2,1)S(1)}, u32[]{:S(2)}, u32[]{:S(2)}) collective-permute-start(bf16[32,2048]{1,0:T(8,128)(2,1)S(1)} %get-tuple-element.6), channel_id=1, source_target_pairs={{0,48},{1,49},{2,50},{3,51},{4,52},{5,53},{6,54},{7,55},{8,24},{9,... | collective-permute-start | bytes 393224 | tf_op jit(solution)/shard_map/ppermute | solution.py:46
  41.8 6.2 %collective-permute-start.8 = (bf16[32,2048]{1,0:T(8,128)(2,1)S(1)}, bf16[32,2048]{1,0:T(8,128)(2,1)S(1)}, u32[]{:S(2)}, u32[]{:S(2)}) collective-permute-start(bf16[32,2048]{1,0:T(8,128)(2,1)S(1)} %collective-permute-done.4), channel_id=1, source_target_pairs={{0,48},{1,49},{2,50},{3,51},{4,52},{5,53},{6,54},{7,55},{8,24},{9,... | collective-permute-start | bytes 393224 | tf_op jit(solution)/shard_map/ppermute | solution.py:46
  42.7 4.5 %collective-permute-start.6 = (bf16[32,2048]{1,0:T(8,128)(2,1)S(1)}, bf16[32,2048]{1,0:T(8,128)(2,1)S(1)}, u32[]{:S(2)}, u32[]{:S(2)}) collective-permute-start(bf16[32,2048]{1,0:T(8,128)(2,1)S(1)} %collective-permute-done.4), channel_id=1, source_target_pairs={{0,16},{1,17},{2,18},{3,19},{4,20},{5,21},{6,22},{7,23},{8,56},{9,... | collective-permute-start | bytes 393224 | tf_op jit(solution)/shard_map/ppermute | solution.py:46
  48.0 18.1 %collective-permute-start.11 = (bf16[6,32,2048]{2,1,0:T(8,128)(2,1)S(1)}, bf16[6,32,2048]{2,1,0:T(8,128)(2,1)S(1)}, u32[]{:S(2)}, u32[]{:S(2)}) collective-permute-start(bf16[6,32,2048]{2,1,0:T(8,128)(2,1)S(1)} %bitcast_dynamic-update-slice_fusion.near_ref), channel_id=1, source_target_pairs={{0,8},{1,9},{2,10},{3,11},{4,12},{5,13},{6,14},{7,15},{8,0},{9,1},... | collective-permute-start | bytes 2359304 | tf_op jit(solution)/shard_map/ppermute | solution.py:46
  53.3 3.8 %collective-permute-start.9 = (bf16[32,2048]{1,0:T(8,128)(2,1)S(1)}, bf16[32,2048]{1,0:T(8,128)(2,1)S(1)}, u32[]{:S(2)}, u32[]{:S(2)}) collective-permute-start(bf16[32,2048]{1,0:T(8,128)(2,1)S(1)} %collective-permute-done.5), channel_id=1, source_target_pairs={{0,16},{1,17},{2,18},{3,19},{4,20},{5,21},{6,22},{7,23},{8,56},{9,... | collective-permute-start | bytes 393224 | tf_op jit(solution)/shard_map/ppermute | solution.py:46
  53.3 6.3 %collective-permute-start.10 = (bf16[32,2048]{1,0:T(8,128)(2,1)S(1)}, bf16[32,2048]{1,0:T(8,128)(2,1)S(1)}, u32[]{:S(2)}, u32[]{:S(2)}) collective-permute-start(bf16[32,2048]{1,0:T(8,128)(2,1)S(1)} %collective-permute-done.6), channel_id=1, source_target_pairs={{0,16},{1,17},{2,18},{3,19},{4,20},{5,21},{6,22},{7,23},{8,56},{9,... | collective-permute-start | bytes 393224 | tf_op jit(solution)/shard_map/ppermute | solution.py:46
  57.1 8.9 %collective-permute-start.12 = (bf16[32,2048]{1,0:T(8,128)(2,1)S(1)}, bf16[32,2048]{1,0:T(8,128)(2,1)S(1)}, u32[]{:S(2)}, u32[]{:S(2)}) collective-permute-start(bf16[32,2048]{1,0:T(8,128)(2,1)S(1)} %collective-permute-done.9.far_0), channel_id=1, source_target_pairs={{0,8},{1,9},{2,10},{3,11},{4,12},{5,13},{6,14},{7,15},{8,0},{9,1},... | collective-permute-start | bytes 393224 | tf_op jit(solution)/shard_map/ppermute | solution.py:46
  59.6 6.5 %collective-permute-start.13 = (bf16[32,2048]{1,0:T(8,128)(2,1)S(1)}, bf16[32,2048]{1,0:T(8,128)(2,1)S(1)}, u32[]{:S(2)}, u32[]{:S(2)}) collective-permute-start(bf16[32,2048]{1,0:T(8,128)(2,1)S(1)} %collective-permute-done.10.far_1), channel_id=1, source_target_pairs={{0,8},{1,9},{2,10},{3,11},{4,12},{5,13},{6,14},{7,15},{8,0},{9,1},... | collective-permute-start | bytes 393224 | tf_op jit(solution)/shard_map/ppermute | solution.py:46
